TPU v7x, 32 devices: a whole 2x2x4 slice. The times are simulated.
32 devices in a mesh: pipe: 4 (over y, x), ctx: 8 (over z, core).
Axes of the slice: x: 2, y: 2, z: 4, core: 2. Of those that a mesh axis runs over, the one named last changes fastest.
Arguments:
- ssm_input: bfloat16 [4, 3072, 4096], P('pipe', 'ctx'), may hold values from -0.078125 to 0.078125
- input_proj: bfloat16 [4, 3072, 512], P('pipe', 'ctx'), may hold values from -0.25 to 0.25
- output_proj: bfloat16 [4, 3072, 512], P('pipe', 'ctx'), may hold values from -0.25 to 0.25
- log_decay: float32 [4, 64, 3072], P('pipe', None, 'ctx'), may hold values from -2 to 0, as said below
- grad_output: bfloat16 [4, 3072, 4096], P('pipe', 'ctx'), may hold values from -6 to 6
- skip_gain: float32 [4, 64], P('pipe'), may hold values from 0.5 to 1.5
Outputs:
- grad_passed: bfloat16 [4, 3072, 4096], P('pipe', 'ctx')
- grad_input_proj: bfloat16 [4, 3072, 512], P('pipe', 'ctx')
- grad_output_proj: bfloat16 [4, 3072, 512], P('pipe', 'ctx')
- grad_decay: float32 [4, 64, 3072], P('pipe', None, 'ctx')
Inputs may be any that keep to these rules, and one draw needn't show every extreme that they name: log_decay is never positive.
All inputs are finite; a program needn't handle non-finite values.
Results may differ from a plain program's by a relative error of at most 0.012.
Values may be sent and summed in bfloat16 or wider, within the bound.
A program may use at most 128 MiB of HBM per device.

v0:
```python
import functools

import jax
import jax.numpy as jnp
from jax import lax
from jax.experimental import pallas as pl
from jax.experimental.pallas import tpu as pltpu
from jax.sharding import PartitionSpec as P

H = 64
P_SIZE = 64
N = 128
G = 4
HPG = 16
W = HPG * P_SIZE
Q = 128
PIECES = 8
LOG2E = 1.4426950408889634
MESH = pl.DeviceIdType.MESH
F32 = jnp.float32
BF16 = jnp.bfloat16


def dot(a, b, ca=1, cb=0):
    return lax.dot_general(a, b, (((ca,), (cb,)), ((), ())), preferred_element_type=F32)


def iota(shape, axis):
    return lax.broadcasted_iota(jnp.int32, shape, axis)


def split3(value):
    high = value.astype(BF16)
    rest = value - high.astype(F32)
    middle = rest.astype(BF16)
    return high, middle, (rest - middle.astype(F32)).astype(BF16)


def ones_where(condition):
    return jnp.where(condition, 1.0, 0.0).astype(BF16)


def spread_matrix():
    shape = (2 * HPG, W)
    return ones_where(iota(shape, 0) % HPG == iota(shape, 1) // P_SIZE)


def spread(weights, matrix):
    high = weights.astype(BF16)
    low = (weights - high.astype(F32)).astype(BF16)
    first = iota(weights.shape, 1) < HPG
    return dot(jnp.where(first, high.astype(F32), low.astype(F32)).astype(BF16), matrix)


def columns_cumulative(decay, lower):
    twice = jnp.concatenate([decay, decay], axis=0)
    return sum(dot(lower, part, 1, 1) for part in split3(twice))


def relay_kernel(n, per, s_ref, a_ref, e_ref, ent_ref, adj_ref, fs, bs, fsend, frecv, bsend, brecv):
    me = lax.axis_index("ctx")
    pipe = lax.axis_index("pipe")
    right, left = lax.rem(me + 1, n), lax.rem(me + n - 1, n)
    barrier = pltpu.get_barrier_semaphore()
    for neighbour in (left, right):
        pl.semaphore_signal(barrier, inc=1, device_id=(pipe, neighbour), device_id_type=MESH)
    pl.semaphore_wait(barrier, 2)

    def forward(k):
        return pltpu.make_async_remote_copy(
            src_ref=fs.at[k], dst_ref=ent_ref.at[k], send_sem=fsend.at[k], recv_sem=frecv.at[k],
            device_id=(pipe, right), device_id_type=MESH)

    def backward(k):
        return pltpu.make_async_remote_copy(
            src_ref=bs.at[k], dst_ref=adj_ref.at[k], send_sem=bsend.at[k], recv_sem=brecv.at[k],
            device_id=(pipe, left), device_id_type=MESH)

    def advance(k, place, make, got, local, sent):
        @pl.when(place > 0)
        def _():
            make(k).wait_recv()

        @pl.when(place == 0)
        def _():
            got[k] = jnp.zeros(got.shape[1:], BF16)

        @pl.when(place < n - 1)
        def _():
            sent[k] = (e_ref[k] * got[k].astype(F32) + local[k].astype(F32)).astype(BF16)
            make(k).start()

    def step(t, carry):
        kf = t - me
        kb = t - (n - 1 - me)

        @pl.when(jnp.logical_and(kf >= 0, kf < PIECES))
        def _():
            advance(kf, me, forward, ent_ref, s_ref, fs)

        @pl.when(jnp.logical_and(kb >= 0, kb < PIECES))
        def _():
            advance(kb, n - 1 - me, backward, adj_ref, a_ref, bs)

        return carry

    lax.fori_loop(0, n + PIECES - 1, step, 0)

    @pl.when(me < n - 1)
    def _():
        for k in range(PIECES):
            forward(k).wait_send()

    @pl.when(me > 0)
    def _():
        for k in range(PIECES):
            backward(k).wait_send()


def group_kernel(x_ref, b_ref, c_ref, decay_ref, g_ref, skip_ref, ent_ref, adj_ref,
                 gx_ref, db_ref, dc_ref, gd_ref,
                 xw_ref, gw_ref, end_ref, es_ref, ds_ref, edge_ref, cq_ref, cqt_ref, mixed_ref, row_ref, col_ref):
    chunks = x_ref.shape[0] // Q
    square = (Q, Q)
    lower = ones_where(iota(square, 1) <= iota(square, 0))
    upper = ones_where(iota(square, 0) <= iota(square, 1))
    matrix = spread_matrix()
    half = ent_ref.shape[2]

    for k in range(W // half):
        es_ref[0, :, k * half : (k + 1) * half] = ent_ref[k]
        ds_ref[chunks - 1, :, k * half : (k + 1) * half] = adj_ref[k]
    col_ref[...] = jnp.zeros(square, F32)
    keep = []
    for c in range(chunks):
        rows = slice(c * Q, (c + 1) * Q)
        decay = decay_ref[:, rows] * LOG2E
        cum = columns_cumulative(decay, lower)
        cqt_ref[c] = cum
        cq_ref[c] = sum(dot(part, upper) for part in split3(decay))
        end = spread(jnp.exp2(cum[Q - 1 : Q, :] - cum), matrix)
        start = spread(jnp.exp2(cum), matrix)
        end_ref[rows, :] = end
        xw_ref[rows, :] = (end * x_ref[rows, :].astype(F32)).astype(BF16)
        gw_ref[rows, :] = (start * g_ref[rows, :].astype(F32)).astype(BF16)
        keep.append(start[Q - 1 : Q, :])
    for c in range(chunks - 1):
        rows = slice(c * Q, (c + 1) * Q)
        local = dot(b_ref[rows, :], xw_ref[rows, :], 0, 0)
        es_ref[c + 1] = (keep[c] * es_ref[c].astype(F32) + local).astype(BF16)
    for c in range(chunks - 1, 0, -1):
        rows = slice(c * Q, (c + 1) * Q)
        local = dot(c_ref[rows, :], gw_ref[rows, :], 0, 0)
        ds_ref[c - 1] = (keep[c] * ds_ref[c].astype(F32) + local).astype(BF16)

    def chunk(c, carry):
        rows = pl.ds(pl.multiple_of(c * Q, Q), Q)
        bc = b_ref[rows, :]
        cc = c_ref[rows, :]
        valid = iota(square, 1) >= iota(square, 0)
        inner = jnp.where(valid, dot(bc, cc, 1, 1), 0.0)
        edge_ref[...] = dot(bc, ds_ref[c])
        cqt = cqt_ref[c]
        low_lane = iota(square, 1) < P_SIZE
        for pair in range(HPG // 2):
            lanes = slice(pair * 128, (pair + 1) * 128)
            xp = x_ref[rows, lanes]
            gp = g_ref[rows, lanes]
            zero = jnp.zeros_like(gp)
            gm = jnp.concatenate([jnp.where(low_lane, gp, zero), jnp.where(low_lane, zero, gp)], axis=0)
            pair_prod = dot(xp, gm, 1, 1)
            inners = []
            mixed = None
            for i in range(2):
                h = 2 * pair + i
                gap = jnp.minimum(cq_ref[c, h : h + 1, :] - cqt[:, h : h + 1], 0.0)
                kernel = jnp.exp2(gap)
                kp = kernel * pair_prod[:, i * Q : (i + 1) * Q]
                mixed = kp if mixed is None else mixed + kp
                inners.append((kernel * inner).astype(BF16))
                joint = kp * inner
                row_ref[h : h + 1, :] = jnp.sum(joint, axis=0, keepdims=True)
                col_ref[:, h : h + 1] = jnp.sum(joint, axis=1, keepdims=True)
            if pair == 0:
                mixed_ref[...] = mixed
            else:
                mixed_ref[...] += mixed
            local = dot(jnp.concatenate(inners, axis=1), gm)
            gx_ref[rows, lanes] = (
                local + end_ref[rows, lanes] * edge_ref[:, lanes] + skip_ref[:, lanes] * gp.astype(F32)
            ).astype(BF16)
        mixed_t = jnp.where(valid, mixed_ref[...], 0.0)
        xw = xw_ref[rows, :]
        gw = gw_ref[rows, :]
        ent = es_ref[c]
        adj = ds_ref[c]
        db_ref[rows, :] = (dot(mixed_t.astype(BF16), cc) + dot(xw, adj, 1, 1)).astype(BF16)
        dc_ref[rows, :] = (dot(mixed_t.T.astype(BF16), bc) + dot(gw, ent, 1, 1)).astype(BF16)
        right = xw.astype(F32) * edge_ref[...]
        left = gw.astype(F32) * dot(cc, ent)
        both = left - right
        high = both.astype(BF16)
        low = (both - high.astype(F32)).astype(BF16)
        heads = ones_where(iota((HPG, W), 0) == iota((HPG, W), 1) // P_SIZE)
        terms = dot(heads, high, 1, 1) + dot(heads, low, 1, 1)
        total = jnp.exp2(cq_ref[c][:, Q - 1 : Q])
        cross = jnp.sum(ent.astype(F32) * adj.astype(F32), axis=0, keepdims=True)
        rights = jnp.sum(right, axis=0, keepdims=True)
        wide = heads.astype(F32)
        last = total * jnp.sum(wide * cross, axis=1, keepdims=True) + jnp.sum(wide * rights, axis=1, keepdims=True)
        grads = row_ref[...] - col_ref[...].T[:HPG, :] + terms
        grads = grads + jnp.where(iota((HPG, Q), 1) == Q - 1, last, 0.0)
        gd_ref[c] = sum(dot(part, lower) for part in split3(grads))
        return carry

    lax.fori_loop(0, chunks, chunk, 0)


def local(ssm_input, input_proj, output_proj, log_decay, grad_output, skip_gain):
    x, b, c, decay, g = ssm_input[0], input_proj[0], output_proj[0], log_decay[0], grad_output[0]
    length = x.shape[0]
    chunks = length // Q
    n = lax.axis_size("ctx")
    half = G * W // PIECES
    skip = jnp.repeat(skip_gain, P_SIZE, axis=1)

    def in_specs(pick):
        return [
            pl.BlockSpec((length, W), lambda i: (0, pick(i))),
            pl.BlockSpec((length, N), lambda i: (0, pick(i))),
            pl.BlockSpec((length, N), lambda i: (0, pick(i))),
            pl.BlockSpec((HPG, length), lambda i: (pick(i), 0)),
            pl.BlockSpec((length, W), lambda i: (0, pick(i))),
        ]

    states = jax.ShapeDtypeStruct((PIECES, N, half), BF16)
    halves = W // half
    state_local, adjoint_local, kept = pl.pallas_call(
        functools.partial(setup_pieces, halves, half),
        grid=(G,),
        in_specs=in_specs(lambda i: i),
        out_specs=[
            pl.BlockSpec((halves, N, half), lambda i: (i, 0, 0)),
            pl.BlockSpec((halves, N, half), lambda i: (i, 0, 0)),
            pl.BlockSpec((halves, 1, half), lambda i: (i, 0, 0)),
        ],
        out_shape=[states, states, jax.ShapeDtypeStruct((PIECES, 1, half), F32)],
        compiler_params=pltpu.CompilerParams(vmem_limit_bytes=48 << 20),
        name="block_states",
    )(x, b, c, decay, g)

    whole = pl.BlockSpec(memory_space=pltpu.VMEM)
    entering, adjoint = pl.pallas_call(
        functools.partial(relay_kernel, n, half),
        in_specs=[whole] * 3,
        out_specs=[whole] * 2,
        out_shape=[states, states],
        scratch_shapes=[pltpu.VMEM((PIECES, N, half), BF16)] * 2 + [pltpu.SemaphoreType.DMA((PIECES,))] * 4,
        compiler_params=pltpu.CompilerParams(collective_id=0, has_side_effects=True, vmem_limit_bytes=32 << 20),
        name="relay",
    )(state_local, adjoint_local, kept)

    devices = lax.axis_size("pipe")
    route = [(source, (source - 1) % devices) for source in range(devices)]
    results = []
    for group in range(G):
        pick = functools.partial(lambda at, i: at, group)
        out = pl.pallas_call(
            group_kernel,
            grid=(1,),
            in_specs=in_specs(pick) + [
                pl.BlockSpec((1, W), lambda i, pick=pick: (0, pick(i))),
                pl.BlockSpec((halves, N, half), lambda i, pick=pick: (pick(i), 0, 0)),
                pl.BlockSpec((halves, N, half), lambda i, pick=pick: (pick(i), 0, 0)),
            ],
            out_specs=[
                pl.BlockSpec((length, W), lambda i: (0, 0)),
                pl.BlockSpec((length, N), lambda i: (0, 0)),
                pl.BlockSpec((length, N), lambda i: (0, 0)),
                pl.BlockSpec((chunks, HPG, Q), lambda i: (0, 0, 0)),
            ],
            out_shape=[
                jax.ShapeDtypeStruct((length, W), BF16),
                jax.ShapeDtypeStruct((length, N), BF16),
                jax.ShapeDtypeStruct((length, N), BF16),
                jax.ShapeDtypeStruct((chunks, HPG, Q), F32),
            ],
            scratch_shapes=[
                pltpu.VMEM((length, W), BF16),
                pltpu.VMEM((length, W), BF16),
                pltpu.VMEM((length, W), F32),
                pltpu.VMEM((chunks, N, W), BF16),
                pltpu.VMEM((chunks, N, W), BF16),
                pltpu.VMEM((Q, W), F32),
                pltpu.VMEM((chunks, HPG, Q), F32),
                pltpu.VMEM((chunks, Q, 2 * HPG), F32),
                pltpu.VMEM((Q, Q), F32),
                pltpu.VMEM((HPG, Q), F32),
                pltpu.VMEM((Q, Q), F32),
            ],
            compiler_params=pltpu.CompilerParams(vmem_limit_bytes=48 << 20),
            cost_estimate=pl.CostEstimate(flops=3_000_000_000, bytes_accessed=4_000_000, transcendentals=1_000_000),
            name="group_grads",
        )(x, b, c, decay, g, skip, entering, adjoint)
        results.append((lax.ppermute(out[0], "pipe", route),) + tuple(out[1:]))
    grad_x = jnp.concatenate([item[0] for item in results], axis=1)
    grad_b = jnp.concatenate([item[1] for item in results], axis=1)
    grad_c = jnp.concatenate([item[2] for item in results], axis=1)
    grad_decay = jnp.concatenate([item[3].transpose(1, 0, 2).reshape(HPG, length) for item in results], axis=0)
    return grad_x[None], grad_b[None], grad_c[None], grad_decay[None]


def setup_pieces(halves, half, x_ref, b_ref, c_ref, decay_ref, g_ref, s_ref, a_ref, e_ref):
    length = x_ref.shape[0]
    shape = (length, length)
    lower = ones_where(iota(shape, 1) <= iota(shape, 0))
    matrix = spread_matrix()
    cum = columns_cumulative(decay_ref[...] * LOG2E, lower)
    end = spread(jnp.exp2(cum[length - 1 : length, :] - cum), matrix)
    start = spread(jnp.exp2(cum), matrix)
    xw = (end * x_ref[...].astype(F32)).astype(BF16)
    gw = (start * g_ref[...].astype(F32)).astype(BF16)
    for k in range(halves):
        lanes = slice(k * half, (k + 1) * half)
        s_ref[k] = dot(b_ref[...], xw[:, lanes], 0, 0).astype(BF16)
        a_ref[k] = dot(c_ref[...], gw[:, lanes], 0, 0).astype(BF16)
        e_ref[k] = start[length - 1 : length, lanes]


def solution(mesh):
    return jax.shard_map(
        local,
        mesh=mesh,
        in_specs=(
            P("pipe", "ctx", None),
            P("pipe", "ctx", None),
            P("pipe", "ctx", None),
            P("pipe", None, "ctx"),
            P("pipe", "ctx", None),
            P("pipe", None),
        ),
        out_specs=(
            P("pipe", "ctx", None),
            P("pipe", "ctx", None),
            P("pipe", "ctx", None),
            P("pipe", None, "ctx"),
        ),
        check_vma=False,
    )
```

profile of v0, /device:TPU:0, one launch (start us, length us, event | category | flops | bytes accessed | tf_op | source)
XLA Modules:
  0.0 130.3 jit_solution(11170257879984475380)
XLA Ops:
  0.6 0.7 broadcast_in_dim.17
  1.4 0.1 broadcast_in_dim.18.skip_ref
  1.5 0.0 copy-start
  1.5 1.9 %copy-done = bf16[1,384,4096]{2,1,0:T(8,128)(2,1)S(1)} copy-done((bf16[1,384,4096]{2,1,0:T(8,128)(2,1)S(1)}, bf16[1,384,4096]{2,1,0:T(8,128)(2,1)}, u32[]{:S(2)}) %copy-start) | copy-done | bytes 3145752
  3.3 0.0 copy-start.1
  3.3 1.0 copy-done.1
  4.3 0.0 copy-start.3
  4.3 1.0 copy-done.3
  5.3 0.0 copy-start.5
  5.3 0.9 copy-done.5
  6.2 0.0 copy-start.2
  6.2 0.0 copy-start.4
  6.2 0.0 copy-start.6
  6.2 6.4 %block_states.1 = (bf16[8,128,512]{2,1,0:T(8,128)(2,1)S(1)}, bf16[8,128,512]{2,1,0:T(8,128)(2,1)S(1)}, f32[8,1,512]{2,1,0:T(1,128)S(1)}) custom-call(bf16[384,4096]{1,0:T(8,128)(2,1)S(1)} %bitcast.42, bf16[384,512]{1,0:T(8,128)(2,1)S(1)} %bitcast.43, bf16[384,512]{1,0:T(8,128)(2,1)S(1)} %bitcast.48, f32[64,384]{1,0:T(8,128)S(1)} %bitcast.53, ...), custom_call_target="tpu_custom_call" | custom-call | tf_op jit(solution)/shard_map/block_states/pallas_call | solution.py:238
  12.6 38.4 %relay.1 = (bf16[8,128,512]{2,1,0:T(8,128)(2,1)S(1)}, bf16[8,128,512]{2,1,0:T(8,128)(2,1)S(1)}) custom-call(bf16[8,128,512]{2,1,0:T(8,128)(2,1)S(1)} %get-tuple-element.25.s_ref, bf16[8,128,512]{2,1,0:T(8,128)(2,1)S(1)} %get-tuple-element.26.a_ref, f32[8,1,512]{2,1,0:T(1,128)S(1)} %get-tuple-element.27.e_ref), custom_call_target="tpu_custom_call" | custom-call | tf_op jit(solution)/shard_map/relay/pallas_call | solution.py:253
  51.1 0.0 copy-done.2
  51.1 0.0 copy-done.4
  51.1 0.0 copy-done.6
  51.1 7.3 %group_grads.7 = (bf16[384,1024]{1,0:T(8,128)(2,1)S(1)}, bf16[384,128]{1,0:T(8,128)(2,1)S(1)}, bf16[384,128]{1,0:T(8,128)(2,1)S(1)}, f32[3,16,128]{2,1,0:T(8,128)S(1)}) custom-call(bf16[384,4096]{1,0:T(8,128)(2,1)} %bitcast.38, bf16[384,512]{1,0:T(8,128)(2,1)S(1)} %bitcast.44, bf16[384,512]{1,0:T(8,128)(2,1)S(1)} %bitcast.49, f32[64,384]{1,0:T(8,128)S(1)} %bitcast.54, ...), custom_call_target="tpu_custom_call" | custom-call | flops 3000000000 | bytes 4000000 | tf_op jit(solution)/shard_map/group_grads/pallas_call | solution.py:268
  58.4 2.5 %collective-permute-start.3 = (bf16[384,1024]{1,0:T(8,128)(2,1)S(1)}, bf16[384,1024]{1,0:T(8,128)(2,1)S(1)}, u32[]{:S(2)}, u32[]{:S(2)}) collective-permute-start(bf16[384,1024]{1,0:T(8,128)(2,1)S(1)} %get-tuple-element.33), channel_id=1, source_target_pairs={{0,24},{8,0},{16,8},{24,16},{1,25},{9,1},{17,9},{25,17},{2,26},{10... | collective-permute-start | bytes 2359304 | tf_op jit(solution)/shard_map/ppermute | solution.py:305
  60.8 7.3 %group_grads.6 = (bf16[384,1024]{1,0:T(8,128)(2,1)S(1)}, bf16[384,128]{1,0:T(8,128)(2,1)S(1)}, bf16[384,128]{1,0:T(8,128)(2,1)S(1)}, f32[3,16,128]{2,1,0:T(8,128)S(1)}) custom-call(bf16[384,4096]{1,0:T(8,128)(2,1)} %bitcast.39, bf16[384,512]{1,0:T(8,128)(2,1)S(1)} %bitcast.45, bf16[384,512]{1,0:T(8,128)(2,1)S(1)} %bitcast.50, f32[64,384]{1,0:T(8,128)S(1)} %bitcast.55, ...), custom_call_target="tpu_custom_call" | custom-call | flops 3000000000 | bytes 4000000 | tf_op jit(solution)/shard_map/group_grads/pallas_call | solution.py:268
  68.1 0.5 collective-permute-start.2
  68.6 7.3 %group_grads.5 = (bf16[384,1024]{1,0:T(8,128)(2,1)S(1)}, bf16[384,128]{1,0:T(8,128)(2,1)S(1)}, bf16[384,128]{1,0:T(8,128)(2,1)S(1)}, f32[3,16,128]{2,1,0:T(8,128)S(1)}) custom-call(bf16[384,4096]{1,0:T(8,128)(2,1)} %bitcast.40, bf16[384,512]{1,0:T(8,128)(2,1)S(1)} %bitcast.46, bf16[384,512]{1,0:T(8,128)(2,1)S(1)} %bitcast.51, f32[64,384]{1,0:T(8,128)S(1)} %bitcast.56, ...), custom_call_target="tpu_custom_call" | custom-call | flops 3000000000 | bytes 4000000 | tf_op jit(solution)/shard_map/group_grads/pallas_call | solution.py:268
  75.9 1.4 %collective-permute-start.1 = (bf16[384,1024]{1,0:T(8,128)(2,1)S(1)}, bf16[384,1024]{1,0:T(8,128)(2,1)S(1)}, u32[]{:S(2)}, u32[]{:S(2)}) collective-permute-start(bf16[384,1024]{1,0:T(8,128)(2,1)S(1)} %get-tuple-element.31), channel_id=1, source_target_pairs={{0,24},{8,0},{16,8},{24,16},{1,25},{9,1},{17,9},{25,17},{2,26},{10... | collective-permute-start | bytes 2359304 | tf_op jit(solution)/shard_map/ppermute | solution.py:305
  77.4 7.3 %group_grads.4 = (bf16[384,1024]{1,0:T(8,128)(2,1)S(1)}, bf16[384,128]{1,0:T(8,128)(2,1)S(1)}, bf16[384,128]{1,0:T(8,128)(2,1)S(1)}, f32[3,16,128]{2,1,0:T(8,128)S(1)}) custom-call(bf16[384,4096]{1,0:T(8,128)(2,1)} %bitcast.41, bf16[384,512]{1,0:T(8,128)(2,1)S(1)} %bitcast.47, bf16[384,512]{1,0:T(8,128)(2,1)S(1)} %bitcast.52, f32[64,384]{1,0:T(8,128)S(1)} %bitcast.57, ...), custom_call_target="tpu_custom_call" | custom-call | flops 3000000000 | bytes 4000000 | tf_op jit(solution)/shard_map/group_grads/pallas_call | solution.py:268
  84.6 0.5 collective-permute-start
  85.2 0.6 maximum_bitcast_fusion.3
  85.8 1.0 maximum_bitcast_fusion.1
  86.8 0.0 collective-permute-done.3
  86.8 8.8 %collective-permute-done.2 = bf16[384,1024]{1,0:T(8,128)(2,1)S(1)} collective-permute-done((bf16[384,1024]{1,0:T(8,128)(2,1)S(1)}, bf16[384,1024]{1,0:T(8,128)(2,1)S(1)}, u32[]{:S(2)}, u32[]{:S(2)}) %collective-permute-start.2) | collective-permute-done | bytes 786464 | tf_op jit(solution)/shard_map/ppermute | solution.py:305
  95.6 16.9 %collective-permute-done.1 = bf16[384,1024]{1,0:T(8,128)(2,1)S(1)} collective-permute-done((bf16[384,1024]{1,0:T(8,128)(2,1)S(1)}, bf16[384,1024]{1,0:T(8,128)(2,1)S(1)}, u32[]{:S(2)}, u32[]{:S(2)}) %collective-permute-start.1) | collective-permute-done | bytes 786464 | tf_op jit(solution)/shard_map/ppermute | solution.py:305
  112.5 16.1 %collective-permute-done = bf16[384,1024]{1,0:T(8,128)(2,1)S(1)} collective-permute-done((bf16[384,1024]{1,0:T(8,128)(2,1)S(1)}, bf16[384,1024]{1,0:T(8,128)(2,1)S(1)}, u32[]{:S(2)}, u32[]{:S(2)}) %collective-permute-start) | collective-permute-done | bytes 786464 | tf_op jit(solution)/shard_map/ppermute | solution.py:305
  128.5 1.8 %maximum_bitcast_fusion = bf16[1,384,4096]{2,1,0:T(8,128)(2,1)} fusion(bf16[384,1024]{1,0:T(8,128)(2,1)S(1)} %collective-permute-done.3, bf16[384,1024]{1,0:T(8,128)(2,1)S(1)} %collective-permute-done.2, bf16[384,1024]{1,0:T(8,128)(2,1)S(1)} %collective-permute-done.1, bf16[384,1024]{1,0:T(8,128)(2,1)S(1)} %collective-permute-done), kind=kLoop, calls=%fused_computation | loop fusion | flops 12582912 | bytes 6291456 | tf_op jit(solution)/shard_map/broadcast_in_dim | solution.py:310
  (2 shorter events, 0.0 us)
Async XLA Ops:
  1.5 1.9 %copy-start = (bf16[1,384,4096]{2,1,0:T(8,128)(2,1)S(1)}, bf16[1,384,4096]{2,1,0:T(8,128)(2,1)}, u32[]{:S(2)}) copy-start(bf16[1,384,4096]{2,1,0:T(8,128)(2,1)} %param.6) | copy-start | bytes 9437188
  3.3 1.0 copy-start.1
  4.3 1.0 copy-start.3
  5.3 0.9 copy-start.5
  6.2 44.8 %copy-start.2 = (bf16[1,384,512]{2,1,0:T(8,128)(2,1)S(1)}, bf16[1,384,512]{2,1,0:T(8,128)(2,1)}, u32[]{:S(2)}) copy-start(bf16[1,384,512]{2,1,0:T(8,128)(2,1)} %param.7) | copy-start | bytes 1179652
  6.2 44.8 %copy-start.4 = (bf16[1,384,512]{2,1,0:T(8,128)(2,1)S(1)}, bf16[1,384,512]{2,1,0:T(8,128)(2,1)}, u32[]{:S(2)}) copy-start(bf16[1,384,512]{2,1,0:T(8,128)(2,1)} %param.8) | copy-start | bytes 1179652
  6.2 44.8 %copy-start.6 = (f32[1,64,384]{2,1,0:T(8,128)S(1)}, f32[1,64,384]{2,1,0:T(8,128)}, u32[]{:S(2)}) copy-start(f32[1,64,384]{2,1,0:T(8,128)} %param.9) | copy-start | bytes 294916
  58.4 28.4 %collective-permute-start.3 = (bf16[384,1024]{1,0:T(8,128)(2,1)S(1)}, bf16[384,1024]{1,0:T(8,128)(2,1)S(1)}, u32[]{:S(2)}, u32[]{:S(2)}) collective-permute-start(bf16[384,1024]{1,0:T(8,128)(2,1)S(1)} %get-tuple-element.33), channel_id=1, source_target_pairs={{0,24},{8,0},{16,8},{24,16},{1,25},{9,1},{17,9},{25,17},{2,26},{10... | collective-permute-start | bytes 2359304 | tf_op jit(solution)/shard_map/ppermute | solution.py:305
  68.1 27.5 %collective-permute-start.2 = (bf16[384,1024]{1,0:T(8,128)(2,1)S(1)}, bf16[384,1024]{1,0:T(8,128)(2,1)S(1)}, u32[]{:S(2)}, u32[]{:S(2)}) collective-permute-start(bf16[384,1024]{1,0:T(8,128)(2,1)S(1)} %get-tuple-element.32), channel_id=1, source_target_pairs={{0,24},{8,0},{16,8},{24,16},{1,25},{9,1},{17,9},{25,17},{2,26},{10... | collective-permute-start | bytes 2359304 | tf_op jit(solution)/shard_map/ppermute | solution.py:305
  75.9 36.6 %collective-permute-start.1 = (bf16[384,1024]{1,0:T(8,128)(2,1)S(1)}, bf16[384,1024]{1,0:T(8,128)(2,1)S(1)}, u32[]{:S(2)}, u32[]{:S(2)}) collective-permute-start(bf16[384,1024]{1,0:T(8,128)(2,1)S(1)} %get-tuple-element.31), channel_id=1, source_target_pairs={{0,24},{8,0},{16,8},{24,16},{1,25},{9,1},{17,9},{25,17},{2,26},{10... | collective-permute-start | bytes 2359304 | tf_op jit(solution)/shard_map/ppermute | solution.py:305
  84.6 43.9 %collective-permute-start = (bf16[384,1024]{1,0:T(8,128)(2,1)S(1)}, bf16[384,1024]{1,0:T(8,128)(2,1)S(1)}, u32[]{:S(2)}, u32[]{:S(2)}) collective-permute-start(bf16[384,1024]{1,0:T(8,128)(2,1)S(1)} %get-tuple-element.30), channel_id=1, source_target_pairs={{0,24},{8,0},{16,8},{24,16},{1,25},{9,1},{17,9},{25,17},{2,26},{10... | collective-permute-start | bytes 2359304 | tf_op jit(solution)/shard_map/ppermute | solution.py:305
where the time goes:
time: 131 us; the launch traced here: 130 us
  Pallas kernels  73.9 us (56%)
  waiting for transfers between devices  41.7 us (32%)
  local copies, waits for them, and re-layouts  5.6 us (4%)
  starting transfers between devices  4.99 us (4%)
  other arithmetic  3.4 us (3%)
    ppermute x4, waiting for transfers between devices, local(): results.append((lax.ppermute(out[0], 'pipe', route),) + tuple(out[1:]))  41.7 us
    pallas_call x1, Pallas kernels, local(): pl.pallas_call(functools.partial(relay_kernel, n, half), in_specs=[whole]...  38.4 us
    pallas_call x4, Pallas kernels, local(): pl.pallas_call(group_kernel, grid=(1,), in_specs=in_specs(pick) + [pl.Blo...  29.1 us
    pallas_call x1, Pallas kernels, local(): pl.pallas_call(functools.partial(setup_pieces, halves, half), grid=(G,),...  6.36 us
    ppermute x4, starting transfers between devices, local(): results.append((lax.ppermute(out[0], 'pipe', route),) + tuple(out[1:]))  4.99 us
    unnamed x14, local copies, waits for them, and re-layouts  4.78 us
    broadcast_in_dim x3, other arithmetic, local(): return (grad_x[None], grad_b[None], grad_c[None], grad_decay[None])  3.4 us
  transfers between devices with their start and end apart: 4, of which 3 were waited for; matrix products, arithmetic and copies ran while one was open for 1% of the time, Pallas kernels for 17%

commit v1 on v0

--- a/solution.py
+++ b/solution.py
@@ -15,6 +15,7 @@
 W = HPG * P_SIZE
 Q = 128
 PIECES = 8
+RAW = 2
 LOG2E = 1.4426950408889634
 MESH = pl.DeviceIdType.MESH
 F32 = jnp.float32
@@ -57,14 +58,57 @@
     return sum(dot(lower, part, 1, 1) for part in split3(twice))
 
 
-def relay_kernel(n, per, s_ref, a_ref, e_ref, ent_ref, adj_ref, fs, bs, fsend, frecv, bsend, brecv):
+def relay_kernel(n, halves, half, x_hbm, b_hbm, c_hbm, decay_hbm, g_hbm, ent_ref, adj_ref,
+                 xv, bv, cv, dv, gv, s_ref, a_ref, e_ref, fs, bs, small_sem, wide_sem, fsend, frecv, bsend, brecv):
     me = lax.axis_index("ctx")
     pipe = lax.axis_index("pipe")
     right, left = lax.rem(me + 1, n), lax.rem(me + n - 1, n)
+    length = x_hbm.shape[0]
+    small = [
+        pltpu.make_async_copy(source, target, small_sem.at[at])
+        for at, (source, target) in enumerate(((decay_hbm, dv), (b_hbm, bv), (c_hbm, cv)))
+    ]
+
+    def wide(group):
+        lanes = pl.ds(pl.multiple_of(group * W, W), W)
+        return (
+            pltpu.make_async_copy(x_hbm.at[:, lanes], xv.at[group], wide_sem.at[0, group]),
+            pltpu.make_async_copy(g_hbm.at[:, lanes], gv.at[group], wide_sem.at[1, group]),
+        )
+
+    for copy in small:
+        copy.start()
+    for group in range(G):
+        for copy in wide(group):
+            copy.start()
     barrier = pltpu.get_barrier_semaphore()
     for neighbour in (left, right):
         pl.semaphore_signal(barrier, inc=1, device_id=(pipe, neighbour), device_id_type=MESH)
-    pl.semaphore_wait(barrier, 2)
+    for copy in small:
+        copy.wait()
+
+    def states(group):
+        for copy in wide(group):
+            copy.wait()
+        shape = (length, length)
+        lower = ones_where(iota(shape, 1) <= iota(shape, 0))
+        matrix = spread_matrix()
+        decay = dv[pl.ds(pl.multiple_of(group * HPG, HPG), HPG), :]
+        cum = columns_cumulative(decay * LOG2E, lower)
+        lanes = pl.ds(pl.multiple_of(group * N, N), N)
+        b = bv[:, lanes]
+        c = cv[:, lanes]
+        end = spread(jnp.exp2(cum[length - 1 : length, :] - cum), matrix)
+        start = spread(jnp.exp2(cum), matrix)
+        xw = (end * xv[group].astype(F32)).astype(BF16)
+        gw = (start * gv[group].astype(F32)).astype(BF16)
+        s = dot(b, xw, 0, 0)
+        a = dot(c, gw, 0, 0)
+        for k in range(halves):
+            cut = slice(k * half, (k + 1) * half)
+            s_ref[group * halves + k] = s[:, cut]
+            a_ref[group * halves + k] = a[:, cut]
+            e_ref[group * halves + k] = start[length - 1 : length, cut]
 
     def forward(k):
         return pltpu.make_async_remote_copy(
@@ -87,12 +131,20 @@
 
         @pl.when(place < n - 1)
         def _():
-            sent[k] = (e_ref[k] * got[k].astype(F32) + local[k].astype(F32)).astype(BF16)
+            sent[k] = (e_ref[k] * got[k].astype(F32) + local[k]).astype(BF16)
             make(k).start()
 
     def step(t, carry):
         kf = t - me
         kb = t - (n - 1 - me)
+
+        @pl.when(jnp.logical_and(lax.rem(t, halves) == 0, t < PIECES))
+        def _():
+            states(lax.div(t, halves))
+
+        @pl.when(t == 0)
+        def _():
+            pl.semaphore_wait(barrier, 2)
 
         @pl.when(jnp.logical_and(kf >= 0, kf < PIECES))
         def _():
@@ -117,9 +169,10 @@
             backward(k).wait_send()
 
 
-def group_kernel(x_ref, b_ref, c_ref, decay_ref, g_ref, skip_ref, ent_ref, adj_ref,
-                 gx_ref, db_ref, dc_ref, gd_ref,
-                 xw_ref, gw_ref, end_ref, es_ref, ds_ref, edge_ref, cq_ref, cqt_ref, mixed_ref, row_ref, col_ref):
+def group_kernel(with_x, x_ref, b_ref, c_ref, decay_ref, g_ref, skip_ref, ent_ref, adj_ref, *refs):
+    if with_x:
+        gx_ref, *refs = refs
+    (db_ref, dc_ref, gd_ref, xw_ref, gw_ref, end_ref, es_ref, ds_ref, edge_ref, cq_ref, cqt_ref, mixed_ref, row_ref, col_ref) = refs
     chunks = x_ref.shape[0] // Q
     square = (Q, Q)
     lower = ones_where(iota(square, 1) <= iota(square, 0))
@@ -177,7 +230,8 @@
                 kernel = jnp.exp2(gap)
                 kp = kernel * pair_prod[:, i * Q : (i + 1) * Q]
                 mixed = kp if mixed is None else mixed + kp
-                inners.append((kernel * inner).astype(BF16))
+                if with_x:
+                    inners.append((kernel * inner).astype(BF16))
                 joint = kp * inner
                 row_ref[h : h + 1, :] = jnp.sum(joint, axis=0, keepdims=True)
                 col_ref[:, h : h + 1] = jnp.sum(joint, axis=1, keepdims=True)
@@ -185,6 +239,8 @@
                 mixed_ref[...] = mixed
             else:
                 mixed_ref[...] += mixed
+            if not with_x:
+                continue
             local = dot(jnp.concatenate(inners, axis=1), gm)
             gx_ref[rows, lanes] = (
                 local + end_ref[rows, lanes] * edge_ref[:, lanes] + skip_ref[:, lanes] * gp.astype(F32)
@@ -216,75 +272,170 @@
     lax.fori_loop(0, chunks, chunk, 0)
 
 
+def pack_kernel(heads, g_ref, b_ref, c_ref, decay_ref, skip_ref, raw_ref, out_ref, sems):
+    g_lanes, b_lanes = heads * P_SIZE, heads // HPG * N
+    copies = [
+        pltpu.make_async_copy(g_ref.at[:, :g_lanes], raw_ref.at[:, :g_lanes], sems.at[0]),
+        pltpu.make_async_copy(b_ref.at[:, :b_lanes], raw_ref.at[:, pl.ds(g_lanes, b_lanes)], sems.at[1]),
+        pltpu.make_async_copy(c_ref.at[:, :b_lanes], raw_ref.at[:, pl.ds(g_lanes + b_lanes, b_lanes)], sems.at[2]),
+    ]
+    for copy in copies:
+        copy.start()
+    length = decay_ref.shape[1]
+    out_ref[:, :length] = decay_ref[:heads, :]
+    own = iota((heads, H), 0) == iota((heads, H), 1)
+    column = jnp.sum(jnp.where(own, skip_ref[...], 0.0), axis=1, keepdims=True)
+    out_ref[:, length:] = jnp.broadcast_to(column, (heads, 128))
+    for copy in copies:
+        copy.wait()
+
+
+def passed_kernel(g_ref, b_ref, c_ref, decay_ref, adj_ref, gx_ref, gw_ref, end_ref, ds_ref, edge_ref, cq_ref, cqt_ref):
+    length = g_ref.shape[0]
+    chunks = length // Q
+    square = (Q, Q)
+    lower = ones_where(iota(square, 1) <= iota(square, 0))
+    upper = ones_where(iota(square, 0) <= iota(square, 1))
+    matrix = spread_matrix()
+    half = adj_ref.shape[2]
+    for k in range(W // half):
+        ds_ref[chunks - 1, :, k * half : (k + 1) * half] = adj_ref[k]
+    wide = ones_where(iota((HPG, W), 0) == iota((HPG, W), 1) // P_SIZE).astype(F32)
+    skip = jnp.sum(wide * decay_ref[:, length : length + 1], axis=0, keepdims=True)
+    keep = []
+    for c in range(chunks):
+        rows = slice(c * Q, (c + 1) * Q)
+        decay = decay_ref[:, rows] * LOG2E
+        cum = columns_cumulative(decay, lower)
+        cqt_ref[c] = cum
+        cq_ref[c] = sum(dot(part, upper) for part in split3(decay))
+        end_ref[rows, :] = spread(jnp.exp2(cum[Q - 1 : Q, :] - cum), matrix)
+        start = spread(jnp.exp2(cum), matrix)
+        gw_ref[rows, :] = (start * g_ref[rows, :].astype(F32)).astype(BF16)
+        keep.append(start[Q - 1 : Q, :])
+    for c in range(chunks - 1, 0, -1):
+        rows = slice(c * Q, (c + 1) * Q)
+        local = dot(c_ref[rows, :], gw_ref[rows, :], 0, 0)
+        ds_ref[c - 1] = (keep[c] * ds_ref[c].astype(F32) + local).astype(BF16)
+
+    def chunk(c, carry):
+        rows = pl.ds(pl.multiple_of(c * Q, Q), Q)
+        bc = b_ref[rows, :]
+        valid = iota(square, 1) >= iota(square, 0)
+        inner = jnp.where(valid, dot(bc, c_ref[rows, :], 1, 1), 0.0)
+        edge_ref[...] = dot(bc, ds_ref[c])
+        cqt = cqt_ref[c]
+        low_lane = iota(square, 1) < P_SIZE
+        for pair in range(HPG // 2):
+            lanes = slice(pair * 128, (pair + 1) * 128)
+            gp = g_ref[rows, lanes]
+            zero = jnp.zeros_like(gp)
+            gm = jnp.concatenate([jnp.where(low_lane, gp, zero), jnp.where(low_lane, zero, gp)], axis=0)
+            inners = []
+            for i in range(2):
+                h = 2 * pair + i
+                gap = jnp.minimum(cq_ref[c, h : h + 1, :] - cqt[:, h : h + 1], 0.0)
+                inners.append((jnp.exp2(gap) * inner).astype(BF16))
+            local = dot(jnp.concatenate(inners, axis=1), gm)
+            gx_ref[rows, lanes] = (
+                local + end_ref[rows, lanes] * edge_ref[:, lanes] + skip[:, lanes] * gp.astype(F32)
+            ).astype(BF16)
+        return carry
+
+    lax.fori_loop(0, chunks, chunk, 0)
+
+
 def local(ssm_input, input_proj, output_proj, log_decay, grad_output, skip_gain):
     x, b, c, decay, g = ssm_input[0], input_proj[0], output_proj[0], log_decay[0], grad_output[0]
     length = x.shape[0]
     chunks = length // Q
     n = lax.axis_size("ctx")
     half = G * W // PIECES
+    halves = W // half
     skip = jnp.repeat(skip_gain, P_SIZE, axis=1)
-
-    def in_specs(pick):
-        return [
-            pl.BlockSpec((length, W), lambda i: (0, pick(i))),
-            pl.BlockSpec((length, N), lambda i: (0, pick(i))),
-            pl.BlockSpec((length, N), lambda i: (0, pick(i))),
-            pl.BlockSpec((HPG, length), lambda i: (pick(i), 0)),
-            pl.BlockSpec((length, W), lambda i: (0, pick(i))),
-        ]
+    devices = lax.axis_size("pipe")
+    route = [(source, (source - 1) % devices) for source in range(devices)]
+
+    def send(value):
+        return lax.ppermute(value, "pipe", route)
+
+    heads = RAW * HPG
+    whole = pl.BlockSpec(memory_space=pltpu.VMEM)
+    away = pl.BlockSpec(memory_space=pl.ANY)
+    raw, raw_decay = pl.pallas_call(
+        functools.partial(pack_kernel, heads),
+        in_specs=[away] * 3 + [whole] * 2,
+        out_specs=[away, whole],
+        out_shape=[
+            jax.ShapeDtypeStruct((length, heads * P_SIZE + 2 * RAW * N), BF16),
+            jax.ShapeDtypeStruct((heads, length + 128), F32),
+        ],
+        scratch_shapes=[pltpu.SemaphoreType.DMA((3,))],
+        compiler_params=pltpu.CompilerParams(vmem_limit_bytes=60 << 20),
+        name="pack_raw",
+    )(g, b, c, decay, skip_gain)
+    raw = send(raw)
+    raw_decay = send(raw_decay)
 
     states = jax.ShapeDtypeStruct((PIECES, N, half), BF16)
-    halves = W // half
-    state_local, adjoint_local, kept = pl.pallas_call(
-        functools.partial(setup_pieces, halves, half),
-        grid=(G,),
-        in_specs=in_specs(lambda i: i),
-        out_specs=[
-            pl.BlockSpec((halves, N, half), lambda i: (i, 0, 0)),
-            pl.BlockSpec((halves, N, half), lambda i: (i, 0, 0)),
-            pl.BlockSpec((halves, 1, half), lambda i: (i, 0, 0)),
-        ],
-        out_shape=[states, states, jax.ShapeDtypeStruct((PIECES, 1, half), F32)],
-        compiler_params=pltpu.CompilerParams(vmem_limit_bytes=48 << 20),
-        name="block_states",
-    )(x, b, c, decay, g)
-
-    whole = pl.BlockSpec(memory_space=pltpu.VMEM)
     entering, adjoint = pl.pallas_call(
-        functools.partial(relay_kernel, n, half),
-        in_specs=[whole] * 3,
+        functools.partial(relay_kernel, n, halves, half),
+        in_specs=[away] * 5,
         out_specs=[whole] * 2,
         out_shape=[states, states],
-        scratch_shapes=[pltpu.VMEM((PIECES, N, half), BF16)] * 2 + [pltpu.SemaphoreType.DMA((PIECES,))] * 4,
-        compiler_params=pltpu.CompilerParams(collective_id=0, has_side_effects=True, vmem_limit_bytes=32 << 20),
+        scratch_shapes=[
+            pltpu.VMEM((G, length, W), BF16),
+            pltpu.VMEM((length, G * N), BF16),
+            pltpu.VMEM((length, G * N), BF16),
+            pltpu.VMEM((H, length), F32),
+            pltpu.VMEM((G, length, W), BF16),
+            pltpu.VMEM((PIECES, N, half), F32),
+            pltpu.VMEM((PIECES, N, half), F32),
+            pltpu.VMEM((PIECES, 1, half), F32),
+            pltpu.VMEM((PIECES, N, half), BF16),
+            pltpu.VMEM((PIECES, N, half), BF16),
+            pltpu.SemaphoreType.DMA((3,)),
+            pltpu.SemaphoreType.DMA((2, G)),
+        ] + [pltpu.SemaphoreType.DMA((PIECES,))] * 4,
+        compiler_params=pltpu.CompilerParams(collective_id=0, has_side_effects=True, vmem_limit_bytes=60 << 20),
+        cost_estimate=pl.CostEstimate(flops=30_000_000_000, bytes_accessed=8_000_000, transcendentals=1_000_000),
         name="relay",
-    )(state_local, adjoint_local, kept)
-
-    devices = lax.axis_size("pipe")
-    route = [(source, (source - 1) % devices) for source in range(devices)]
-    results = []
-    for group in range(G):
-        pick = functools.partial(lambda at, i: at, group)
-        out = pl.pallas_call(
-            group_kernel,
+    )(x, b, c, decay, g)
+    raw_adjoint = send(adjoint[: RAW * halves])
+
+    def own_group(group, with_x):
+        pick = lambda i: (0, group)
+        rows = lambda i: (group, 0)
+        pieces = pl.BlockSpec((halves, N, half), lambda i: (group, 0, 0))
+        flat = lambda i: (0, 0)
+        out_specs = [
+            pl.BlockSpec((length, W), flat),
+            pl.BlockSpec((length, N), flat),
+            pl.BlockSpec((length, N), flat),
+            pl.BlockSpec((chunks, HPG, Q), lambda i: (0, 0, 0)),
+        ]
+        out_shape = [
+            jax.ShapeDtypeStruct((length, W), BF16),
+            jax.ShapeDtypeStruct((length, N), BF16),
+            jax.ShapeDtypeStruct((length, N), BF16),
+            jax.ShapeDtypeStruct((chunks, HPG, Q), F32),
+        ]
+        first = 0 if with_x else 1
+        return pl.pallas_call(
+            functools.partial(group_kernel, with_x),
             grid=(1,),
-            in_specs=in_specs(pick) + [
-                pl.BlockSpec((1, W), lambda i, pick=pick: (0, pick(i))),
-                pl.BlockSpec((halves, N, half), lambda i, pick=pick: (pick(i), 0, 0)),
-                pl.BlockSpec((halves, N, half), lambda i, pick=pick: (pick(i), 0, 0)),
+            in_specs=[
+                pl.BlockSpec((length, W), pick),
+                pl.BlockSpec((length, N), pick),
+                pl.BlockSpec((length, N), pick),
+                pl.BlockSpec((HPG, length), rows),
+                pl.BlockSpec((length, W), pick),
+                pl.BlockSpec((1, W), pick),
+                pieces,
+                pieces,
             ],
-            out_specs=[
-                pl.BlockSpec((length, W), lambda i: (0, 0)),
-                pl.BlockSpec((length, N), lambda i: (0, 0)),
-                pl.BlockSpec((length, N), lambda i: (0, 0)),
-                pl.BlockSpec((chunks, HPG, Q), lambda i: (0, 0, 0)),
-            ],
-            out_shape=[
-                jax.ShapeDtypeStruct((length, W), BF16),
-                jax.ShapeDtypeStruct((length, N), BF16),
-                jax.ShapeDtypeStruct((length, N), BF16),
-                jax.ShapeDtypeStruct((chunks, HPG, Q), F32),
-            ],
+            out_specs=out_specs[first:],
+            out_shape=out_shape[first:],
             scratch_shapes=[
                 pltpu.VMEM((length, W), BF16),
                 pltpu.VMEM((length, W), BF16),
@@ -298,33 +449,47 @@
                 pltpu.VMEM((HPG, Q), F32),
                 pltpu.VMEM((Q, Q), F32),
             ],
-            compiler_params=pltpu.CompilerParams(vmem_limit_bytes=48 << 20),
+            compiler_params=pltpu.CompilerParams(vmem_limit_bytes=60 << 20),
             cost_estimate=pl.CostEstimate(flops=3_000_000_000, bytes_accessed=4_000_000, transcendentals=1_000_000),
             name="group_grads",
         )(x, b, c, decay, g, skip, entering, adjoint)
-        results.append((lax.ppermute(out[0], "pipe", route),) + tuple(out[1:]))
-    grad_x = jnp.concatenate([item[0] for item in results], axis=1)
-    grad_b = jnp.concatenate([item[1] for item in results], axis=1)
-    grad_c = jnp.concatenate([item[2] for item in results], axis=1)
-    grad_decay = jnp.concatenate([item[3].transpose(1, 0, 2).reshape(HPG, length) for item in results], axis=0)
+
+    sent = {}
+    rest = {}
+    for group in list(range(RAW, G)) + list(range(RAW)):
+        out = own_group(group, group >= RAW)
+        if group >= RAW:
+            sent[group] = send(out[0])
+        rest[group] = out[-3:]
+    passed_first = pl.pallas_call(
+        passed_kernel,
+        grid=(RAW,),
+        in_specs=[
+            pl.BlockSpec((length, W), lambda i: (0, i)),
+            pl.BlockSpec((length, N), lambda i: (0, RAW * (W // N) + i)),
+            pl.BlockSpec((length, N), lambda i: (0, RAW * (W // N) + RAW + i)),
+            pl.BlockSpec((HPG, length + 128), lambda i: (i, 0)),
+            pl.BlockSpec((halves, N, half), lambda i: (i, 0, 0)),
+        ],
+        out_specs=pl.BlockSpec((length, W), lambda i: (0, i)),
+        out_shape=jax.ShapeDtypeStruct((length, RAW * W), BF16),
+        scratch_shapes=[
+            pltpu.VMEM((length, W), BF16),
+            pltpu.VMEM((length, W), F32),
+            pltpu.VMEM((chunks, N, W), BF16),
+            pltpu.VMEM((Q, W), F32),
+            pltpu.VMEM((chunks, HPG, Q), F32),
+            pltpu.VMEM((chunks, Q, 2 * HPG), F32),
+        ],
+        compiler_params=pltpu.CompilerParams(vmem_limit_bytes=60 << 20),
+        cost_estimate=pl.CostEstimate(flops=4_000_000_000, bytes_accessed=4_000_000, transcendentals=1_000_000),
+        name="passed_grads",
+    )(raw, raw, raw, raw_decay, raw_adjoint)
+    grad_x = jnp.concatenate([passed_first] + [sent[group] for group in range(RAW, G)], axis=1)
+    grad_b = jnp.concatenate([rest[group][0] for group in range(G)], axis=1)
+    grad_c = jnp.concatenate([rest[group][1] for group in range(G)], axis=1)
+    grad_decay = jnp.concatenate([rest[group][2].transpose(1, 0, 2).reshape(HPG, length) for group in range(G)], axis=0)
     return grad_x[None], grad_b[None], grad_c[None], grad_decay[None]
-
-
-def setup_pieces(halves, half, x_ref, b_ref, c_ref, decay_ref, g_ref, s_ref, a_ref, e_ref):
-    length = x_ref.shape[0]
-    shape = (length, length)
-    lower = ones_where(iota(shape, 1) <= iota(shape, 0))
-    matrix = spread_matrix()
-    cum = columns_cumulative(decay_ref[...] * LOG2E, lower)
-    end = spread(jnp.exp2(cum[length - 1 : length, :] - cum), matrix)
-    start = spread(jnp.exp2(cum), matrix)
-    xw = (end * x_ref[...].astype(F32)).astype(BF16)
-    gw = (start * g_ref[...].astype(F32)).astype(BF16)
-    for k in range(halves):
-        lanes = slice(k * half, (k + 1) * half)
-        s_ref[k] = dot(b_ref[...], xw[:, lanes], 0, 0).astype(BF16)
-        a_ref[k] = dot(c_ref[...], gw[:, lanes], 0, 0).astype(BF16)
-        e_ref[k] = start[length - 1 : length, lanes]
 
 
 def solution(mesh):

time: 131 us -> 166 us (1.27)
  Pallas kernels: 73.9 us -> 146 us
  waiting for transfers between devices: 41.7 us -> 0.01 us
  starting transfers between devices: 4.99 us -> 8.94 us
  local copies, waits for them, and re-layouts: 5.6 us -> 3.44 us
  other arithmetic: 3.4 us -> 5.52 us
    pallas_call x6 -> x7, Pallas kernels: 73.9 us -> 146 us  [the longest x1 62.2 us: local(): pl.pallas_call(functools.partial(pack_kernel, heads), in_specs=[away] * 3...]
    ppermute x4 -> x5, waiting for transfers between devices: 41.7 us -> 0.01 us  [send(): return lax.ppermute(value, 'pipe', route)]
    ppermute x4 -> x5, starting transfers between devices: 4.99 us -> 8.94 us  [send(): return lax.ppermute(value, 'pipe', route)]
    unnamed x14 -> x24, local copies, waits for them, and re-layouts: 4.78 us -> 0.86 us
    broadcast_in_dim x3, other arithmetic: 3.4 us -> 5.52 us  [local(): return (grad_x[None], grad_b[None], grad_c[None], grad_decay[None])]
  transfers between devices with their start and end apart: 4 -> 5, of which waited for: 3 -> 0; matrix products, arithmetic and copies ran while one was open for 1% -> 3% of each run, Pallas kernels for 17% -> 51%
where the time goes in v1:
time: 166 us; the launch traced here: 165 us
  Pallas kernels  146 us (88%)
  starting transfers between devices  8.94 us (5%)
  other arithmetic  5.52 us (3%)
  local copies, waits for them, and re-layouts  3.44 us (2%)
    pallas_call x1, Pallas kernels, local(): pl.pallas_call(functools.partial(pack_kernel, heads), in_specs=[away] * 3...  62.2 us
    pallas_call x1, Pallas kernels, local(): pl.pallas_call(functools.partial(relay_kernel, n, halves, half), in_specs...  41.8 us
    pallas_call x4, Pallas kernels, own_group(): pl.pallas_call(functools.partial(group_kernel, with_x), grid=(1,), in_spe...  33.8 us
    ppermute x5, starting transfers between devices, send(): return lax.ppermute(value, 'pipe', route)  8.94 us
    pallas_call x1, Pallas kernels, local(): pl.pallas_call(passed_kernel, grid=(RAW,), in_specs=[pl.BlockSpec((length...  8.66 us
    broadcast_in_dim x3, other arithmetic, local(): return (grad_x[None], grad_b[None], grad_c[None], grad_decay[None])  5.52 us
  transfers between devices with their start and end apart: 5, of which 0 were waited for; matrix products, arithmetic and copies ran while one was open for 3% of the time, Pallas kernels for 51%

profile of v1, /device:TPU:0, one launch (start us, length us, event | category | flops | bytes accessed | tf_op | source)
XLA Modules:
  0.0 165.1 jit_solution(3808762390276259293)
XLA Ops:
  0.6 62.2 %pack_raw.1 = (bf16[384,2560]{1,0:T(8,128)(2,1)}, f32[32,512]{1,0:T(8,128)}) custom-call(bf16[384,4096]{1,0:T(8,128)(2,1)} %bitcast.38, bf16[384,512]{1,0:T(8,128)(2,1)} %bitcast.44, bf16[384,512]{1,0:T(8,128)(2,1)} %bitcast.50, f32[64,384]{1,0:T(8,128)} %bitcast.56, f32[1,64]{1,0:T(1,128)} %skip_ref.1), custom_call_target="tpu_custom_call" | custom-call | tf_op jit(solution)/shard_map/pack_raw/pallas_call | solution.py:365
  62.8 3.9 %collective-permute-start.1 = (f32[32,512]{1,0:T(8,128)}, f32[32,512]{1,0:T(8,128)S(1)}, u32[]{:S(2)}, u32[]{:S(2)}) collective-permute-start(f32[32,512]{1,0:T(8,128)} %get-tuple-element.23), channel_id=1, source_target_pairs={{0,24},{8,0},{16,8},{24,16},{1,25},{9,1},{17,9},{25,17},{2,26},{10... | collective-permute-start | bytes 196616 | tf_op jit(solution)/shard_map/ppermute | solution.py:360
  66.8 0.5 collective-permute-start
  67.3 0.0 copy-start.9
  67.3 41.8 %relay.1 = (bf16[8,128,512]{2,1,0:T(8,128)(2,1)}, bf16[8,128,512]{2,1,0:T(8,128)(2,1)}) custom-call(bf16[384,4096]{1,0:T(8,128)(2,1)} %bitcast.63, bf16[384,512]{1,0:T(8,128)(2,1)} %bitcast.45, bf16[384,512]{1,0:T(8,128)(2,1)} %bitcast.51, f32[64,384]{1,0:T(8,128)} %bitcast.57, bf16[384,4096]{1,0:T(8,128)(2,1)} %bitcast.39), custom_call_target="tpu_custom_call" | custom-call | flops 30000001024 | bytes 8000000 | tf_op jit(solution)/shard_map/relay/pallas_call | solution.py:381
  109.2 1.1 slice.3
  110.2 1.5 collective-permute-start.2
  111.7 0.0 copy-done.9
  111.7 0.1 broadcast_in_dim.17
  111.8 0.7 broadcast_in_dim.18.skip_ref
  112.5 8.2 %group_grads.5 = (bf16[384,1024]{1,0:T(8,128)(2,1)}, bf16[384,128]{1,0:T(8,128)(2,1)}, bf16[384,128]{1,0:T(8,128)(2,1)}, f32[3,16,128]{2,1,0:T(8,128)}) custom-call(bf16[384,4096]{1,0:T(8,128)(2,1)} %bitcast.64, bf16[384,512]{1,0:T(8,128)(2,1)} %bitcast.46, bf16[384,512]{1,0:T(8,128)(2,1)} %bitcast.52, f32[64,384]{1,0:T(8,128)} %bitcast.58, ...), custom_call_target="tpu_custom_call" | custom-call | flops 3000000000 | bytes 4000000 | tf_op jit(solution)/shard_map/group_grads/pallas_call | solution.py:424
  120.7 0.1 collective-permute-start.4
  120.8 8.2 %group_grads.4 = (bf16[384,1024]{1,0:T(8,128)(2,1)}, bf16[384,128]{1,0:T(8,128)(2,1)}, bf16[384,128]{1,0:T(8,128)(2,1)}, f32[3,16,128]{2,1,0:T(8,128)}) custom-call(bf16[384,4096]{1,0:T(8,128)(2,1)} %bitcast.65, bf16[384,512]{1,0:T(8,128)(2,1)} %bitcast.47, bf16[384,512]{1,0:T(8,128)(2,1)} %bitcast.53, f32[64,384]{1,0:T(8,128)} %bitcast.59, ...), custom_call_target="tpu_custom_call" | custom-call | flops 3000000000 | bytes 4000000 | tf_op jit(solution)/shard_map/group_grads/pallas_call | solution.py:424
  129.0 2.9 %collective-permute-start.3 = (bf16[384,1024]{1,0:T(8,128)(2,1)}, bf16[384,1024]{1,0:T(8,128)(2,1)S(1)}, u32[]{:S(2)}, u32[]{:S(2)}) collective-permute-start(bf16[384,1024]{1,0:T(8,128)(2,1)} %get-tuple-element.26), channel_id=1, source_target_pairs={{0,24},{8,0},{16,8},{24,16},{1,25},{9,1},{17,9},{25,17},{2,26},{10... | collective-permute-start | bytes 2359304 | tf_op jit(solution)/shard_map/ppermute | solution.py:360
  131.9 8.6 %group_grads.7 = (bf16[384,128]{1,0:T(8,128)(2,1)}, bf16[384,128]{1,0:T(8,128)(2,1)}, f32[3,16,128]{2,1,0:T(8,128)}) custom-call(bf16[384,4096]{1,0:T(8,128)(2,1)} %bitcast.66, bf16[384,512]{1,0:T(8,128)(2,1)} %bitcast.48, bf16[384,512]{1,0:T(8,128)(2,1)} %bitcast.54, f32[64,384]{1,0:T(8,128)} %bitcast.60, bf16[384,4096]{1,0:T(8,128)(2,1)} %bitcast.42, ...), custom_call_target="tpu_custom_call" | custom-call | flops 3000000000 | bytes 4000000 | tf_op jit(solution)/shard_map/group_grads/pallas_call | solution.py:424
  140.5 0.0 copy-start.8
  140.5 0.0 copy-start
  140.5 0.0 copy-start.1
  140.5 0.0 copy-start.2
  140.5 0.0 copy-start.3
  140.5 0.0 copy-start.4
  140.5 0.0 copy-start.5
  140.5 0.0 copy-start.6
  140.6 0.0 copy-start.7
  140.6 8.7 %group_grads.6 = (bf16[384,128]{1,0:T(8,128)(2,1)}, bf16[384,128]{1,0:T(8,128)(2,1)}, f32[3,16,128]{2,1,0:T(8,128)}) custom-call(bf16[384,4096]{1,0:T(8,128)(2,1)} %bitcast.67, bf16[384,512]{1,0:T(8,128)(2,1)} %bitcast.49, bf16[384,512]{1,0:T(8,128)(2,1)} %bitcast.55, f32[64,384]{1,0:T(8,128)} %bitcast.61, bf16[384,4096]{1,0:T(8,128)(2,1)} %bitcast.43, ...), custom_call_target="tpu_custom_call" | custom-call | flops 3000000000 | bytes 4000000 | tf_op jit(solution)/shard_map/group_grads/pallas_call | solution.py:424
  149.3 0.0 copy-done.8
  149.3 0.7 copy_bitcast_fusion.2
  150.0 0.0 copy-done
  150.0 0.0 copy-done.1
  150.1 0.0 copy-done.2
  150.1 0.0 copy-done.3
  150.1 0.0 copy-done.4
  150.1 0.0 copy-done.5
  150.1 1.9 %maximum_bitcast_fusion.1 = (bf16[1,384,512]{2,1,0:T(8,128)(2,1)}, bf16[1,384,512]{2,1,0:T(8,128)(2,1)}) fusion(bf16[384,128]{1,0:T(8,128)(2,1)S(1)} %copy-done, bf16[384,128]{1,0:T(8,128)(2,1)S(1)} %copy-done.2, bf16[384,128]{1,0:T(8,128)(2,1)S(1)} %copy-done.4, bf16[384,128]{1,0:T(8,128)(2,1)} %get-tuple-element.28, bf16[384,128]{1,0:T(8,128)(2,1)S(1)} %copy-done.1, ...), kind=kLoop, calls=%fused_computation.1 | loop fusion | flops 3145728 | bytes 1572864 | tf_op jit(solution)/shard_map/broadcast_in_dim | solution.py:492
  152.0 0.0 copy-done.6
  152.0 0.0 copy-done.7
  152.0 0.7 maximum_bitcast_fusion.3
  152.7 0.0 collective-permute-done.1.decay_ref
  152.7 0.0 copy-start.11
  152.7 0.0 collective-permute-done.2.adj_ref
  152.7 0.0 copy-start.10
  152.7 0.0 collective-permute-done.g_ref.b_ref.c_ref
  152.7 0.6 copy-done.11
  153.3 0.2 copy-done.10
  153.5 8.7 %passed_grads.1 = bf16[384,2048]{1,0:T(8,128)(2,1)} custom-call(bf16[384,2560]{1,0:T(8,128)(2,1)} %collective-permute-done.g_ref.b_ref.c_ref, bf16[384,2560]{1,0:T(8,128)(2,1)} %collective-permute-done.g_ref.b_ref.c_ref, bf16[384,2560]{1,0:T(8,128)(2,1)} %collective-permute-done.g_ref.b_ref.c_ref, f32[32,512]{1,0:T(8,128)} %copy-done.11, ...), custom_call_target="tpu_custom_call" | custom-call | flops 4000000000 | bytes 4000000 | tf_op jit(solution)/shard_map/passed_grads/pallas_call | solution.py:464
  162.2 0.0 collective-permute-done.4
  162.2 0.0 collective-permute-done.3
  162.2 3.0 %maximum_bitcast_fusion = bf16[1,384,4096]{2,1,0:T(8,128)(2,1)} fusion(bf16[384,1024]{1,0:T(8,128)(2,1)S(1)} %collective-permute-done.4, bf16[384,1024]{1,0:T(8,128)(2,1)S(1)} %collective-permute-done.3, bf16[384,2048]{1,0:T(8,128)(2,1)} %passed_grads.1), kind=kLoop, calls=%fused_computation | loop fusion | flops 9437184 | bytes 6291456 | tf_op jit(solution)/shard_map/broadcast_in_dim | solution.py:492
  (1 shorter events, 0.0 us)
Async XLA Ops:
  62.8 89.8 %collective-permute-start.1 = (f32[32,512]{1,0:T(8,128)}, f32[32,512]{1,0:T(8,128)S(1)}, u32[]{:S(2)}, u32[]{:S(2)}) collective-permute-start(f32[32,512]{1,0:T(8,128)} %get-tuple-element.23), channel_id=1, source_target_pairs={{0,24},{8,0},{16,8},{24,16},{1,25},{9,1},{17,9},{25,17},{2,26},{10... | collective-permute-start | bytes 196616 | tf_op jit(solution)/shard_map/ppermute | solution.py:360
  66.8 85.9 %collective-permute-start = (bf16[384,2560]{1,0:T(8,128)(2,1)}, bf16[384,2560]{1,0:T(8,128)(2,1)}, u32[]{:S(2)}, u32[]{:S(2)}) collective-permute-start(bf16[384,2560]{1,0:T(8,128)(2,1)} %get-tuple-element.22), channel_id=1, source_target_pairs={{0,24},{8,0},{16,8},{24,16},{1,25},{9,1},{17,9},{25,17},{2,26},{10... | collective-permute-start | bytes 5898248 | tf_op jit(solution)/shard_map/ppermute | solution.py:360
  67.3 44.4 %copy-start.9 = (f32[1,64]{1,0:T(1,128)S(1)}, f32[1,64]{1,0:T(1,128)}, u32[]{:S(2)}) copy-start(f32[1,64]{1,0:T(1,128)} %skip_ref.1) | copy-start | bytes 772
  110.2 42.4 %collective-permute-start.2 = (bf16[4,128,512]{2,1,0:T(8,128)(2,1)S(1)}, bf16[4,128,512]{2,1,0:T(8,128)(2,1)S(1)}, u32[]{:S(2)}, u32[]{:S(2)}) collective-permute-start(bf16[4,128,512]{2,1,0:T(8,128)(2,1)S(1)} %slice.3), channel_id=1, source_target_pairs={{0,24},{8,0},{16,8},{24,16},{1,25},{9,1},{17,9},{25,17},{2,26},{10... | collective-permute-start | bytes 1572872 | tf_op jit(solution)/shard_map/ppermute | solution.py:360
  120.7 41.5 %collective-permute-start.4 = (bf16[384,1024]{1,0:T(8,128)(2,1)}, bf16[384,1024]{1,0:T(8,128)(2,1)S(1)}, u32[]{:S(2)}, u32[]{:S(2)}) collective-permute-start(bf16[384,1024]{1,0:T(8,128)(2,1)} %get-tuple-element.27), channel_id=1, source_target_pairs={{0,24},{8,0},{16,8},{24,16},{1,25},{9,1},{17,9},{25,17},{2,26},{10... | collective-permute-start | bytes 2359304 | tf_op jit(solution)/shard_map/ppermute | solution.py:360
  129.0 33.2 %collective-permute-start.3 = (bf16[384,1024]{1,0:T(8,128)(2,1)}, bf16[384,1024]{1,0:T(8,128)(2,1)S(1)}, u32[]{:S(2)}, u32[]{:S(2)}) collective-permute-start(bf16[384,1024]{1,0:T(8,128)(2,1)} %get-tuple-element.26), channel_id=1, source_target_pairs={{0,24},{8,0},{16,8},{24,16},{1,25},{9,1},{17,9},{25,17},{2,26},{10... | collective-permute-start | bytes 2359304 | tf_op jit(solution)/shard_map/ppermute | solution.py:360
  140.5 8.8 %copy-start.8 = (f32[3,16,128]{2,1,0:T(8,128)S(1)}, f32[3,16,128]{2,1,0:T(8,128)}, u32[]{:S(2)}) copy-start(f32[3,16,128]{2,1,0:T(8,128)} %get-tuple-element.37) | copy-start | bytes 73732
  140.5 9.6 %copy-start = (bf16[384,128]{1,0:T(8,128)(2,1)S(1)}, bf16[384,128]{1,0:T(8,128)(2,1)}, u32[]{:S(2)}) copy-start(bf16[384,128]{1,0:T(8,128)(2,1)} %get-tuple-element.31) | copy-start | bytes 294916
  140.5 9.6 %copy-start.1 = (bf16[384,128]{1,0:T(8,128)(2,1)S(1)}, bf16[384,128]{1,0:T(8,128)(2,1)}, u32[]{:S(2)}) copy-start(bf16[384,128]{1,0:T(8,128)(2,1)} %get-tuple-element.35) | copy-start | bytes 294916
  140.5 9.6 %copy-start.2 = (bf16[384,128]{1,0:T(8,128)(2,1)S(1)}, bf16[384,128]{1,0:T(8,128)(2,1)}, u32[]{:S(2)}) copy-start(bf16[384,128]{1,0:T(8,128)(2,1)} %get-tuple-element.30) | copy-start | bytes 294916
  140.5 9.6 %copy-start.3 = (bf16[384,128]{1,0:T(8,128)(2,1)S(1)}, bf16[384,128]{1,0:T(8,128)(2,1)}, u32[]{:S(2)}) copy-start(bf16[384,128]{1,0:T(8,128)(2,1)} %get-tuple-element.34) | copy-start | bytes 294916
  140.5 9.6 %copy-start.4 = (bf16[384,128]{1,0:T(8,128)(2,1)S(1)}, bf16[384,128]{1,0:T(8,128)(2,1)}, u32[]{:S(2)}) copy-start(bf16[384,128]{1,0:T(8,128)(2,1)} %get-tuple-element.29) | copy-start | bytes 294916
  140.5 9.6 %copy-start.5 = (bf16[384,128]{1,0:T(8,128)(2,1)S(1)}, bf16[384,128]{1,0:T(8,128)(2,1)}, u32[]{:S(2)}) copy-start(bf16[384,128]{1,0:T(8,128)(2,1)} %get-tuple-element.33) | copy-start | bytes 294916
  140.5 11.5 %copy-start.6 = (f32[3,16,128]{2,1,0:T(8,128)S(1)}, f32[3,16,128]{2,1,0:T(8,128)}, u32[]{:S(2)}) copy-start(f32[3,16,128]{2,1,0:T(8,128)} %get-tuple-element.39) | copy-start | bytes 73732
  140.6 11.5 %copy-start.7 = (f32[3,16,128]{2,1,0:T(8,128)S(1)}, f32[3,16,128]{2,1,0:T(8,128)}, u32[]{:S(2)}) copy-start(f32[3,16,128]{2,1,0:T(8,128)} %get-tuple-element.38) | copy-start | bytes 73732
  152.7 0.6 copy-start.11
  152.7 0.8 copy-start.10

commit v2 on v1

--- a/solution.py
+++ b/solution.py
@@ -58,8 +58,8 @@
     return sum(dot(lower, part, 1, 1) for part in split3(twice))
 
 
-def relay_kernel(n, halves, half, x_hbm, b_hbm, c_hbm, decay_hbm, g_hbm, ent_ref, adj_ref,
-                 xv, bv, cv, dv, gv, s_ref, a_ref, e_ref, fs, bs, small_sem, wide_sem, fsend, frecv, bsend, brecv):
+def relay_kernel(n, halves, half, x_hbm, b_hbm, c_hbm, decay_hbm, g_hbm, ent_ref, adj_ref, gx_ref, db_ref, dc_ref, diff_ref,
+                 mixed_ref, row_ref, col_ref, xv, bv, cv, dv, gv, s_ref, a_ref, e_ref, fs, bs, small_sem, wide_sem, fsend, frecv, bsend, brecv):
     me = lax.axis_index("ctx")
     pipe = lax.axis_index("pipe")
     right, left = lax.rem(me + 1, n), lax.rem(me + n - 1, n)
@@ -110,115 +110,27 @@
             a_ref[group * halves + k] = a[:, cut]
             e_ref[group * halves + k] = start[length - 1 : length, cut]
 
-    def forward(k):
-        return pltpu.make_async_remote_copy(
-            src_ref=fs.at[k], dst_ref=ent_ref.at[k], send_sem=fsend.at[k], recv_sem=frecv.at[k],
-            device_id=(pipe, right), device_id_type=MESH)
-
-    def backward(k):
-        return pltpu.make_async_remote_copy(
-            src_ref=bs.at[k], dst_ref=adj_ref.at[k], send_sem=bsend.at[k], recv_sem=brecv.at[k],
-            device_id=(pipe, left), device_id_type=MESH)
-
-    def advance(k, place, make, got, local, sent):
-        @pl.when(place > 0)
-        def _():
-            make(k).wait_recv()
-
-        @pl.when(place == 0)
-        def _():
-            got[k] = jnp.zeros(got.shape[1:], BF16)
-
-        @pl.when(place < n - 1)
-        def _():
-            sent[k] = (e_ref[k] * got[k].astype(F32) + local[k]).astype(BF16)
-            make(k).start()
-
-    def step(t, carry):
-        kf = t - me
-        kb = t - (n - 1 - me)
-
-        @pl.when(jnp.logical_and(lax.rem(t, halves) == 0, t < PIECES))
-        def _():
-            states(lax.div(t, halves))
-
-        @pl.when(t == 0)
-        def _():
-            pl.semaphore_wait(barrier, 2)
-
-        @pl.when(jnp.logical_and(kf >= 0, kf < PIECES))
-        def _():
-            advance(kf, me, forward, ent_ref, s_ref, fs)
-
-        @pl.when(jnp.logical_and(kb >= 0, kb < PIECES))
-        def _():
-            advance(kb, n - 1 - me, backward, adj_ref, a_ref, bs)
-
-        return carry
-
-    lax.fori_loop(0, n + PIECES - 1, step, 0)
-
-    @pl.when(me < n - 1)
-    def _():
-        for k in range(PIECES):
-            forward(k).wait_send()
-
-    @pl.when(me > 0)
-    def _():
-        for k in range(PIECES):
-            backward(k).wait_send()
-
-
-def group_kernel(with_x, x_ref, b_ref, c_ref, decay_ref, g_ref, skip_ref, ent_ref, adj_ref, *refs):
-    if with_x:
-        gx_ref, *refs = refs
-    (db_ref, dc_ref, gd_ref, xw_ref, gw_ref, end_ref, es_ref, ds_ref, edge_ref, cq_ref, cqt_ref, mixed_ref, row_ref, col_ref) = refs
-    chunks = x_ref.shape[0] // Q
-    square = (Q, Q)
-    lower = ones_where(iota(square, 1) <= iota(square, 0))
-    upper = ones_where(iota(square, 0) <= iota(square, 1))
-    matrix = spread_matrix()
-    half = ent_ref.shape[2]
-
-    for k in range(W // half):
-        es_ref[0, :, k * half : (k + 1) * half] = ent_ref[k]
-        ds_ref[chunks - 1, :, k * half : (k + 1) * half] = adj_ref[k]
-    col_ref[...] = jnp.zeros(square, F32)
-    keep = []
-    for c in range(chunks):
-        rows = slice(c * Q, (c + 1) * Q)
-        decay = decay_ref[:, rows] * LOG2E
-        cum = columns_cumulative(decay, lower)
-        cqt_ref[c] = cum
-        cq_ref[c] = sum(dot(part, upper) for part in split3(decay))
-        end = spread(jnp.exp2(cum[Q - 1 : Q, :] - cum), matrix)
-        start = spread(jnp.exp2(cum), matrix)
-        end_ref[rows, :] = end
-        xw_ref[rows, :] = (end * x_ref[rows, :].astype(F32)).astype(BF16)
-        gw_ref[rows, :] = (start * g_ref[rows, :].astype(F32)).astype(BF16)
-        keep.append(start[Q - 1 : Q, :])
-    for c in range(chunks - 1):
-        rows = slice(c * Q, (c + 1) * Q)
-        local = dot(b_ref[rows, :], xw_ref[rows, :], 0, 0)
-        es_ref[c + 1] = (keep[c] * es_ref[c].astype(F32) + local).astype(BF16)
-    for c in range(chunks - 1, 0, -1):
-        rows = slice(c * Q, (c + 1) * Q)
-        local = dot(c_ref[rows, :], gw_ref[rows, :], 0, 0)
-        ds_ref[c - 1] = (keep[c] * ds_ref[c].astype(F32) + local).astype(BF16)
-
-    def chunk(c, carry):
+    chunks = length // Q
+    col_ref[...] = jnp.zeros((Q, Q), F32)
+
+    def unit(group, c):
+        square = (Q, Q)
+        lower = ones_where(iota(square, 1) <= iota(square, 0))
+        upper = ones_where(iota(square, 0) <= iota(square, 1))
         rows = pl.ds(pl.multiple_of(c * Q, Q), Q)
-        bc = b_ref[rows, :]
-        cc = c_ref[rows, :]
+        lanes_n = pl.ds(pl.multiple_of(group * N, N), N)
+        decay = dv[pl.ds(pl.multiple_of(group * HPG, HPG), HPG), rows] * LOG2E
+        cqt = columns_cumulative(decay, lower)
+        cq = sum(dot(part, upper) for part in split3(decay))
+        bc = bv[rows, lanes_n]
+        cc = cv[rows, lanes_n]
         valid = iota(square, 1) >= iota(square, 0)
         inner = jnp.where(valid, dot(bc, cc, 1, 1), 0.0)
-        edge_ref[...] = dot(bc, ds_ref[c])
-        cqt = cqt_ref[c]
         low_lane = iota(square, 1) < P_SIZE
         for pair in range(HPG // 2):
             lanes = slice(pair * 128, (pair + 1) * 128)
-            xp = x_ref[rows, lanes]
-            gp = g_ref[rows, lanes]
+            xp = xv[group, rows, lanes]
+            gp = gv[group, rows, lanes]
             zero = jnp.zeros_like(gp)
             gm = jnp.concatenate([jnp.where(low_lane, gp, zero), jnp.where(low_lane, zero, gp)], axis=0)
             pair_prod = dot(xp, gm, 1, 1)
@@ -226,12 +138,10 @@
             mixed = None
             for i in range(2):
                 h = 2 * pair + i
-                gap = jnp.minimum(cq_ref[c, h : h + 1, :] - cqt[:, h : h + 1], 0.0)
-                kernel = jnp.exp2(gap)
+                kernel = jnp.exp2(jnp.minimum(cq[h : h + 1, :] - cqt[:, h : h + 1], 0.0))
                 kp = kernel * pair_prod[:, i * Q : (i + 1) * Q]
                 mixed = kp if mixed is None else mixed + kp
-                if with_x:
-                    inners.append((kernel * inner).astype(BF16))
+                inners.append((kernel * inner).astype(BF16))
                 joint = kp * inner
                 row_ref[h : h + 1, :] = jnp.sum(joint, axis=0, keepdims=True)
                 col_ref[:, h : h + 1] = jnp.sum(joint, axis=1, keepdims=True)
@@ -239,55 +149,141 @@
                 mixed_ref[...] = mixed
             else:
                 mixed_ref[...] += mixed
-            if not with_x:
-                continue
-            local = dot(jnp.concatenate(inners, axis=1), gm)
-            gx_ref[rows, lanes] = (
-                local + end_ref[rows, lanes] * edge_ref[:, lanes] + skip_ref[:, lanes] * gp.astype(F32)
-            ).astype(BF16)
+            gx_ref[group, rows, lanes] = dot(jnp.concatenate(inners, axis=1), gm).astype(BF16)
         mixed_t = jnp.where(valid, mixed_ref[...], 0.0)
-        xw = xw_ref[rows, :]
-        gw = gw_ref[rows, :]
+        db_ref[rows, lanes_n] = dot(mixed_t.astype(BF16), cc)
+        dc_ref[rows, lanes_n] = dot(mixed_t.T.astype(BF16), bc)
+        diff_ref[group * chunks + c] = row_ref[...] - col_ref[...].T[:HPG, :]
+
+    def forward(k):
+        return pltpu.make_async_remote_copy(
+            src_ref=fs.at[k], dst_ref=ent_ref.at[k], send_sem=fsend.at[k], recv_sem=frecv.at[k],
+            device_id=(pipe, right), device_id_type=MESH)
+
+    def backward(k):
+        return pltpu.make_async_remote_copy(
+            src_ref=bs.at[k], dst_ref=adj_ref.at[k], send_sem=bsend.at[k], recv_sem=brecv.at[k],
+            device_id=(pipe, left), device_id_type=MESH)
+
+    def advance(k, place, make, got, local, sent):
+        @pl.when(place > 0)
+        def _():
+            make(k).wait_recv()
+
+        @pl.when(place == 0)
+        def _():
+            got[k] = jnp.zeros(got.shape[1:], BF16)
+
+        @pl.when(place < n - 1)
+        def _():
+            sent[k] = (e_ref[k] * got[k].astype(F32) + local[k]).astype(BF16)
+            make(k).start()
+
+    def step(t, carry):
+        kf = t - me
+        kb = t - (n - 1 - me)
+
+        @pl.when(jnp.logical_and(lax.rem(t, halves) == 0, t < PIECES))
+        def _():
+            states(lax.div(t, halves))
+
+        @pl.when(t == 0)
+        def _():
+            pl.semaphore_wait(barrier, 2)
+
+        @pl.when(jnp.logical_and(kf >= 0, kf < PIECES))
+        def _():
+            advance(kf, me, forward, ent_ref, s_ref, fs)
+
+        @pl.when(jnp.logical_and(kb >= 0, kb < PIECES))
+        def _():
+            advance(kb, n - 1 - me, backward, adj_ref, a_ref, bs)
+
+        @pl.when(t < G * chunks)
+        def _():
+            unit(lax.div(t, chunks), lax.rem(t, chunks))
+
+        return carry
+
+    lax.fori_loop(0, max(n + PIECES - 1, G * chunks), step, 0)
+
+    @pl.when(me < n - 1)
+    def _():
+        for k in range(PIECES):
+            forward(k).wait_send()
+
+    @pl.when(me > 0)
+    def _():
+        for k in range(PIECES):
+            backward(k).wait_send()
+
+
+def group_kernel(with_x, x_ref, b_ref, c_ref, decay_ref, g_ref, skip_ref, ent_ref, adj_ref,
+                 near_db_ref, near_dc_ref, diff_ref, *refs):
+    if with_x:
+        near_gx_ref, gx_ref, *refs = refs
+    db_ref, dc_ref, gd_ref, es_ref, ds_ref = refs
+    chunks = x_ref.shape[0] // Q
+    square = (Q, Q)
+    lower = ones_where(iota(square, 1) <= iota(square, 0))
+    matrix = spread_matrix()
+    heads = ones_where(iota((HPG, W), 0) == iota((HPG, W), 1) // P_SIZE)
+    wide = heads.astype(F32)
+    half = ent_ref.shape[2]
+
+    for k in range(W // half):
+        es_ref[0, :, k * half : (k + 1) * half] = ent_ref[k]
+        ds_ref[chunks - 1, :, k * half : (k + 1) * half] = adj_ref[k]
+    spans = [slice(c * Q, (c + 1) * Q) for c in range(chunks)]
+    ends, xws, gws, keep = [], [], [], []
+    for rows in spans:
+        cum = columns_cumulative(decay_ref[:, rows] * LOG2E, lower)
+        end = spread(jnp.exp2(cum[Q - 1 : Q, :] - cum), matrix)
+        start = spread(jnp.exp2(cum), matrix)
+        ends.append(end)
+        xws.append((end * x_ref[rows, :].astype(F32)).astype(BF16))
+        gws.append((start * g_ref[rows, :].astype(F32)).astype(BF16))
+        keep.append(start[Q - 1 : Q, :])
+    for c in range(chunks - 1):
+        near = dot(b_ref[spans[c], :], xws[c], 0, 0)
+        es_ref[c + 1] = (keep[c] * es_ref[c].astype(F32) + near).astype(BF16)
+    for c in range(chunks - 1, 0, -1):
+        near = dot(c_ref[spans[c], :], gws[c], 0, 0)
+        ds_ref[c - 1] = (keep[c] * ds_ref[c].astype(F32) + near).astype(BF16)
+    for c, rows in enumerate(spans):
         ent = es_ref[c]
         adj = ds_ref[c]
-        db_ref[rows, :] = (dot(mixed_t.astype(BF16), cc) + dot(xw, adj, 1, 1)).astype(BF16)
-        dc_ref[rows, :] = (dot(mixed_t.T.astype(BF16), bc) + dot(gw, ent, 1, 1)).astype(BF16)
-        right = xw.astype(F32) * edge_ref[...]
-        left = gw.astype(F32) * dot(cc, ent)
+        edge = dot(b_ref[rows, :], adj)
+        if with_x:
+            gx_ref[rows, :] = (
+                near_gx_ref[0, rows, :].astype(F32) + ends[c] * edge + skip_ref[...] * g_ref[rows, :].astype(F32)
+            ).astype(BF16)
+        db_ref[rows, :] = (near_db_ref[rows, :] + dot(xws[c], adj, 1, 1)).astype(BF16)
+        dc_ref[rows, :] = (near_dc_ref[rows, :] + dot(gws[c], ent, 1, 1)).astype(BF16)
+        right = xws[c].astype(F32) * edge
+        left = gws[c].astype(F32) * dot(c_ref[rows, :], ent)
         both = left - right
         high = both.astype(BF16)
         low = (both - high.astype(F32)).astype(BF16)
-        heads = ones_where(iota((HPG, W), 0) == iota((HPG, W), 1) // P_SIZE)
         terms = dot(heads, high, 1, 1) + dot(heads, low, 1, 1)
-        total = jnp.exp2(cq_ref[c][:, Q - 1 : Q])
-        cross = jnp.sum(ent.astype(F32) * adj.astype(F32), axis=0, keepdims=True)
+        cross = keep[c] * jnp.sum(ent.astype(F32) * adj.astype(F32), axis=0, keepdims=True)
         rights = jnp.sum(right, axis=0, keepdims=True)
-        wide = heads.astype(F32)
-        last = total * jnp.sum(wide * cross, axis=1, keepdims=True) + jnp.sum(wide * rights, axis=1, keepdims=True)
-        grads = row_ref[...] - col_ref[...].T[:HPG, :] + terms
+        last = jnp.sum(wide * (cross + rights), axis=1, keepdims=True)
+        grads = diff_ref[c] + terms
         grads = grads + jnp.where(iota((HPG, Q), 1) == Q - 1, last, 0.0)
-        gd_ref[c] = sum(dot(part, lower) for part in split3(grads))
-        return carry
-
-    lax.fori_loop(0, chunks, chunk, 0)
-
-
-def pack_kernel(heads, g_ref, b_ref, c_ref, decay_ref, skip_ref, raw_ref, out_ref, sems):
+        gd_ref[:, rows] = sum(dot(part, lower) for part in split3(grads))
+
+
+def pack_kernel(heads, g_ref, b_ref, c_ref, decay_ref, skip_ref, raw_ref, out_ref):
     g_lanes, b_lanes = heads * P_SIZE, heads // HPG * N
-    copies = [
-        pltpu.make_async_copy(g_ref.at[:, :g_lanes], raw_ref.at[:, :g_lanes], sems.at[0]),
-        pltpu.make_async_copy(b_ref.at[:, :b_lanes], raw_ref.at[:, pl.ds(g_lanes, b_lanes)], sems.at[1]),
-        pltpu.make_async_copy(c_ref.at[:, :b_lanes], raw_ref.at[:, pl.ds(g_lanes + b_lanes, b_lanes)], sems.at[2]),
-    ]
-    for copy in copies:
-        copy.start()
+    raw_ref[:, :g_lanes] = g_ref[...]
+    raw_ref[:, g_lanes : g_lanes + b_lanes] = b_ref[...]
+    raw_ref[:, g_lanes + b_lanes :] = c_ref[...]
     length = decay_ref.shape[1]
-    out_ref[:, :length] = decay_ref[:heads, :]
+    out_ref[:, :length] = decay_ref[...]
     own = iota((heads, H), 0) == iota((heads, H), 1)
     column = jnp.sum(jnp.where(own, skip_ref[...], 0.0), axis=1, keepdims=True)
     out_ref[:, length:] = jnp.broadcast_to(column, (heads, 128))
-    for copy in copies:
-        copy.wait()
 
 
 def passed_kernel(g_ref, b_ref, c_ref, decay_ref, adj_ref, gx_ref, gw_ref, end_ref, ds_ref, edge_ref, cq_ref, cqt_ref):
@@ -364,13 +360,22 @@
     away = pl.BlockSpec(memory_space=pl.ANY)
     raw, raw_decay = pl.pallas_call(
         functools.partial(pack_kernel, heads),
-        in_specs=[away] * 3 + [whole] * 2,
-        out_specs=[away, whole],
+        grid=(1,),
+        in_specs=[
+            pl.BlockSpec((length, RAW * W), lambda i: (0, 0)),
+            pl.BlockSpec((length, RAW * N), lambda i: (0, 0)),
+            pl.BlockSpec((length, RAW * N), lambda i: (0, 0)),
+            pl.BlockSpec((heads, length), lambda i: (0, 0)),
+            pl.BlockSpec((1, H), lambda i: (0, 0)),
+        ],
+        out_specs=[
+            pl.BlockSpec((length, heads * P_SIZE + 2 * RAW * N), lambda i: (0, 0)),
+            pl.BlockSpec((heads, length + 128), lambda i: (0, 0)),
+        ],
         out_shape=[
             jax.ShapeDtypeStruct((length, heads * P_SIZE + 2 * RAW * N), BF16),
             jax.ShapeDtypeStruct((heads, length + 128), F32),
         ],
-        scratch_shapes=[pltpu.SemaphoreType.DMA((3,))],
         compiler_params=pltpu.CompilerParams(vmem_limit_bytes=60 << 20),
         name="pack_raw",
     )(g, b, c, decay, skip_gain)
@@ -378,12 +383,22 @@
     raw_decay = send(raw_decay)
 
     states = jax.ShapeDtypeStruct((PIECES, N, half), BF16)
-    entering, adjoint = pl.pallas_call(
+    entering, adjoint, near_gx, near_db, near_dc, diff = pl.pallas_call(
         functools.partial(relay_kernel, n, halves, half),
         in_specs=[away] * 5,
-        out_specs=[whole] * 2,
-        out_shape=[states, states],
+        out_specs=[whole] * 6,
+        out_shape=[
+            states,
+            states,
+            jax.ShapeDtypeStruct((G, length, W), BF16),
+            jax.ShapeDtypeStruct((length, G * N), F32),
+            jax.ShapeDtypeStruct((length, G * N), F32),
+            jax.ShapeDtypeStruct((G * chunks, HPG, Q), F32),
+        ],
         scratch_shapes=[
+            pltpu.VMEM((Q, Q), F32),
+            pltpu.VMEM((HPG, Q), F32),
+            pltpu.VMEM((Q, Q), F32),
             pltpu.VMEM((G, length, W), BF16),
             pltpu.VMEM((length, G * N), BF16),
             pltpu.VMEM((length, G * N), BF16),
@@ -412,13 +427,13 @@
             pl.BlockSpec((length, W), flat),
             pl.BlockSpec((length, N), flat),
             pl.BlockSpec((length, N), flat),
-            pl.BlockSpec((chunks, HPG, Q), lambda i: (0, 0, 0)),
+            pl.BlockSpec((HPG, length), flat),
         ]
         out_shape = [
             jax.ShapeDtypeStruct((length, W), BF16),
             jax.ShapeDtypeStruct((length, N), BF16),
             jax.ShapeDtypeStruct((length, N), BF16),
-            jax.ShapeDtypeStruct((chunks, HPG, Q), F32),
+            jax.ShapeDtypeStruct((HPG, length), F32),
         ]
         first = 0 if with_x else 1
         return pl.pallas_call(
@@ -433,26 +448,17 @@
                 pl.BlockSpec((1, W), pick),
                 pieces,
                 pieces,
-            ],
+                pl.BlockSpec((length, N), pick),
+                pl.BlockSpec((length, N), pick),
+                pl.BlockSpec((chunks, HPG, Q), lambda i: (group, 0, 0)),
+            ] + [pl.BlockSpec((1, length, W), lambda i: (group, 0, 0))] * with_x,
             out_specs=out_specs[first:],
             out_shape=out_shape[first:],
-            scratch_shapes=[
-                pltpu.VMEM((length, W), BF16),
-                pltpu.VMEM((length, W), BF16),
-                pltpu.VMEM((length, W), F32),
-                pltpu.VMEM((chunks, N, W), BF16),
-                pltpu.VMEM((chunks, N, W), BF16),
-                pltpu.VMEM((Q, W), F32),
-                pltpu.VMEM((chunks, HPG, Q), F32),
-                pltpu.VMEM((chunks, Q, 2 * HPG), F32),
-                pltpu.VMEM((Q, Q), F32),
-                pltpu.VMEM((HPG, Q), F32),
-                pltpu.VMEM((Q, Q), F32),
-            ],
+            scratch_shapes=[pltpu.VMEM((chunks, N, W), BF16), pltpu.VMEM((chunks, N, W), BF16)],
             compiler_params=pltpu.CompilerParams(vmem_limit_bytes=60 << 20),
             cost_estimate=pl.CostEstimate(flops=3_000_000_000, bytes_accessed=4_000_000, transcendentals=1_000_000),
             name="group_grads",
-        )(x, b, c, decay, g, skip, entering, adjoint)
+        )(x, b, c, decay, g, skip, entering, adjoint, near_db, near_dc, diff, *[near_gx][: int(with_x)])
 
     sent = {}
     rest = {}
@@ -488,7 +494,7 @@
     grad_x = jnp.concatenate([passed_first] + [sent[group] for group in range(RAW, G)], axis=1)
     grad_b = jnp.concatenate([rest[group][0] for group in range(G)], axis=1)
     grad_c = jnp.concatenate([rest[group][1] for group in range(G)], axis=1)
-    grad_decay = jnp.concatenate([rest[group][2].transpose(1, 0, 2).reshape(HPG, length) for group in range(G)], axis=0)
+    grad_decay = jnp.concatenate([rest[group][2] for group in range(G)], axis=0)
     return grad_x[None], grad_b[None], grad_c[None], grad_decay[None]
 
 

time: 166 us -> 110 us (0.66)
  Pallas kernels: 146 us -> 84.6 us
  waiting for transfers between devices: 0.01 us -> 5.93 us
    pallas_call x1, Pallas kernels: 62.2 us -> 2.97 us  [local(): pl.pallas_call(functools.partial(pack_kernel, heads), grid=(1,), in_specs...]
    pallas_call x4, Pallas kernels: 33.8 us -> 24.5 us  [own_group(): pl.pallas_call(functools.partial(group_kernel, with_x), grid=(1,), in_spe...]
    pallas_call x1, Pallas kernels: 41.8 us -> 48.4 us  [local(): pl.pallas_call(functools.partial(relay_kernel, n, halves, half), in_specs...]
    ppermute x5, waiting for transfers between devices: 0.01 us -> 5.93 us  [send(): return lax.ppermute(value, 'pipe', route)]
  transfers between devices with their start and end apart: 5 -> 5, of which waited for: 0 -> 1; matrix products, arithmetic and copies ran while one was open for 3% -> 5% of each run, Pallas kernels for 51% -> 75%
where the time goes in v2:
time: 110 us; the launch traced here: 109 us
  Pallas kernels  84.6 us (77%)
  starting transfers between devices  8.88 us (8%)
  other arithmetic  6.25 us (6%)
  waiting for transfers between devices  5.93 us (5%)
  local copies, waits for them, and re-layouts  2.68 us (2%)
    pallas_call x1, Pallas kernels, local(): pl.pallas_call(functools.partial(relay_kernel, n, halves, half), in_specs...  48.4 us
    pallas_call x4, Pallas kernels, own_group(): pl.pallas_call(functools.partial(group_kernel, with_x), grid=(1,), in_spe...  24.5 us
    ppermute x5, starting transfers between devices, send(): return lax.ppermute(value, 'pipe', route)  8.88 us
    pallas_call x1, Pallas kernels, local(): pl.pallas_call(passed_kernel, grid=(RAW,), in_specs=[pl.BlockSpec((length...  8.67 us
    broadcast_in_dim x3, other arithmetic, local(): return (grad_x[None], grad_b[None], grad_c[None], grad_decay[None])  6.25 us
    ppermute x5, waiting for transfers between devices, send(): return lax.ppermute(value, 'pipe', route)  5.93 us
    pallas_call x1, Pallas kernels, local(): pl.pallas_call(functools.partial(pack_kernel, heads), grid=(1,), in_specs...  2.97 us
  transfers between devices with their start and end apart: 5, of which 1 were waited for; matrix products, arithmetic and copies ran while one was open for 5% of the time, Pallas kernels for 75%

profile of v2, /device:TPU:0, one launch (start us, length us, event | category | flops | bytes accessed | tf_op | source)
XLA Modules:
  0.0 109.1 jit_solution(9769380065652452101)
XLA Ops:
  0.6 3.0 %pack_raw.1 = (bf16[384,2560]{1,0:T(8,128)(2,1)}, f32[32,512]{1,0:T(8,128)}) custom-call(bf16[384,4096]{1,0:T(8,128)(2,1)} %bitcast.14, bf16[384,512]{1,0:T(8,128)(2,1)} %bitcast.25, bf16[384,512]{1,0:T(8,128)(2,1)} %bitcast.31, f32[64,384]{1,0:T(8,128)} %bitcast.37, f32[1,64]{1,0:T(1,128)} %skip_ref.1), custom_call_target="tpu_custom_call" | custom-call | tf_op jit(solution)/shard_map/pack_raw/pallas_call | solution.py:361
  3.6 3.9 %collective-permute-start = (bf16[384,2560]{1,0:T(8,128)(2,1)}, bf16[384,2560]{1,0:T(8,128)(2,1)}, u32[]{:S(2)}, u32[]{:S(2)}) collective-permute-start(bf16[384,2560]{1,0:T(8,128)(2,1)} %get-tuple-element.26), channel_id=1, source_target_pairs={{0,24},{8,0},{16,8},{24,16},{1,25},{9,1},{17,9},{25,17},{2,26},{10... | collective-permute-start | bytes 5898248 | tf_op jit(solution)/shard_map/ppermute | solution.py:356
  7.5 0.0 copy-start.11
  7.5 0.0 copy-start.9
  7.5 48.4 %relay.1 = (bf16[8,128,512]{2,1,0:T(8,128)(2,1)}, bf16[8,128,512]{2,1,0:T(8,128)(2,1)}, bf16[4,384,1024]{2,1,0:T(8,128)(2,1)}, f32[384,512]{1,0:T(8,128)}, f32[384,512]{1,0:T(8,128)}, /*index=5*/f32[12,16,128]{2,1,0:T(8,128)}) custom-call(bf16[384,4096]{1,0:T(8,128)(2,1)} %bitcast.20, bf16[384,512]{1,0:T(8,128)(2,1)} %bitcast.26, bf16[384,512]{1,0:T(8,128)(2,1)} %bitcast.32, ...), custom_call_target="tpu_custom_call" | custom-call | flops 30000001024 | bytes 8000000 | tf_op jit(solution)/shard_map/relay/pallas_call | solution.py:386
  56.0 1.1 slice.3
  57.0 1.0 collective-permute-start.2
  58.0 0.0 copy-done.11
  58.0 1.0 collective-permute-start.1
  59.1 0.0 copy-done.9
  59.1 0.1 broadcast_in_dim.17
  59.1 0.7 broadcast_in_dim.18.skip_ref
  59.8 6.3 %group_grads.4 = (bf16[384,1024]{1,0:T(8,128)(2,1)}, bf16[384,128]{1,0:T(8,128)(2,1)}, bf16[384,128]{1,0:T(8,128)(2,1)}, f32[16,384]{1,0:T(8,128)}) custom-call(bf16[384,4096]{1,0:T(8,128)(2,1)} %bitcast.21, bf16[384,512]{1,0:T(8,128)(2,1)} %bitcast.27, bf16[384,512]{1,0:T(8,128)(2,1)} %bitcast.33, f32[64,384]{1,0:T(8,128)} %bitcast.39, ...), custom_call_target="tpu_custom_call" | custom-call | flops 3000000000 | bytes 4000000 | tf_op jit(solution)/shard_map/group_grads/pallas_call | solution.py:439
  66.1 0.9 collective-permute-start.3
  67.1 6.3 %group_grads.5 = (bf16[384,1024]{1,0:T(8,128)(2,1)}, bf16[384,128]{1,0:T(8,128)(2,1)}, bf16[384,128]{1,0:T(8,128)(2,1)}, f32[16,384]{1,0:T(8,128)}) custom-call(bf16[384,4096]{1,0:T(8,128)(2,1)} %bitcast.22, bf16[384,512]{1,0:T(8,128)(2,1)} %bitcast.28, bf16[384,512]{1,0:T(8,128)(2,1)} %bitcast.34, f32[64,384]{1,0:T(8,128)} %bitcast.40, ...), custom_call_target="tpu_custom_call" | custom-call | flops 3000000000 | bytes 4000000 | tf_op jit(solution)/shard_map/group_grads/pallas_call | solution.py:439
  73.4 2.0 %collective-permute-start.4 = (bf16[384,1024]{1,0:T(8,128)(2,1)}, bf16[384,1024]{1,0:T(8,128)(2,1)S(1)}, u32[]{:S(2)}, u32[]{:S(2)}) collective-permute-start(bf16[384,1024]{1,0:T(8,128)(2,1)} %get-tuple-element.35), channel_id=1, source_target_pairs={{0,24},{8,0},{16,8},{24,16},{1,25},{9,1},{17,9},{25,17},{2,26},{10... | collective-permute-start | bytes 2359304 | tf_op jit(solution)/shard_map/ppermute | solution.py:356
  75.4 5.9 %group_grads.6 = (bf16[384,128]{1,0:T(8,128)(2,1)}, bf16[384,128]{1,0:T(8,128)(2,1)}, f32[16,384]{1,0:T(8,128)}) custom-call(bf16[384,4096]{1,0:T(8,128)(2,1)} %bitcast.23, bf16[384,512]{1,0:T(8,128)(2,1)} %bitcast.29, bf16[384,512]{1,0:T(8,128)(2,1)} %bitcast.35, f32[64,384]{1,0:T(8,128)} %bitcast.41, bf16[384,4096]{1,0:T(8,128)(2,1)} %bitcast.18, ...), custom_call_target="tpu_custom_call" | custom-call | flops 3000000000 | bytes 4000000 | tf_op jit(solution)/shard_map/group_grads/pallas_call | solution.py:439
  81.3 0.0 copy-start
  81.3 0.0 copy-start.1
  81.3 0.0 copy-start.2
  81.3 0.0 copy-start.3
  81.3 0.0 copy-start.4
  81.3 0.0 copy-start.5
  81.3 0.0 copy-start.6
  81.4 0.0 copy-start.7
  81.4 0.0 copy-start.8
  81.4 6.0 %group_grads.7 = (bf16[384,128]{1,0:T(8,128)(2,1)}, bf16[384,128]{1,0:T(8,128)(2,1)}, f32[16,384]{1,0:T(8,128)}) custom-call(bf16[384,4096]{1,0:T(8,128)(2,1)} %bitcast.24, bf16[384,512]{1,0:T(8,128)(2,1)} %bitcast.30, bf16[384,512]{1,0:T(8,128)(2,1)} %bitcast.36, f32[64,384]{1,0:T(8,128)} %bitcast.42, bf16[384,4096]{1,0:T(8,128)(2,1)} %bitcast.19, ...), custom_call_target="tpu_custom_call" | custom-call | flops 3000000000 | bytes 4000000 | tf_op jit(solution)/shard_map/group_grads/pallas_call | solution.py:439
  87.4 0.0 copy-done
  87.4 0.0 copy-done.1
  87.4 0.0 copy-done.2
  87.4 0.0 copy-done.3
  87.4 0.0 copy-done.4
  87.4 0.0 copy-done.5
  87.4 1.9 %maximum_bitcast_fusion.1 = (bf16[1,384,512]{2,1,0:T(8,128)(2,1)}, bf16[1,384,512]{2,1,0:T(8,128)(2,1)}) fusion(bf16[384,128]{1,0:T(8,128)(2,1)S(1)} %copy-done.2, bf16[384,128]{1,0:T(8,128)(2,1)S(1)} %copy-done, bf16[384,128]{1,0:T(8,128)(2,1)} %get-tuple-element.37, bf16[384,128]{1,0:T(8,128)(2,1)S(1)} %copy-done.4, bf16[384,128]{1,0:T(8,128)(2,1)S(1)} %copy-done.3, ...), kind=kLoop, calls=%fused_computation.1 | loop fusion | flops 3145728 | bytes 1572864 | tf_op jit(solution)/shard_map/broadcast_in_dim | solution.py:498
  89.3 0.0 copy-done.6
  89.3 0.0 copy-done.7
  89.3 0.0 copy-done.8
  89.3 1.4 %maximum_bitcast_fusion.3 = f32[1,64,384]{2,1,0:T(8,128)} fusion(f32[16,384]{1,0:T(8,128)S(1)} %copy-done.7, f32[16,384]{1,0:T(8,128)S(1)} %copy-done.6, f32[16,384]{1,0:T(8,128)} %get-tuple-element.45, f32[16,384]{1,0:T(8,128)S(1)} %copy-done.8), kind=kLoop, calls=%fused_computation.3 | loop fusion | flops 73728 | bytes 196608 | tf_op jit(solution)/shard_map/broadcast_in_dim | solution.py:498
  90.7 0.0 collective-permute-done.1.decay_ref
  90.7 0.0 collective-permute-done.2.adj_ref
  90.7 0.0 copy-start.10
  90.8 0.0 collective-permute-done.g_ref.b_ref.c_ref
  90.8 0.6 copy-done.12
  91.4 0.2 copy-done.10
  91.6 8.7 %passed_grads.1 = bf16[384,2048]{1,0:T(8,128)(2,1)} custom-call(bf16[384,2560]{1,0:T(8,128)(2,1)} %collective-permute-done.g_ref.b_ref.c_ref, bf16[384,2560]{1,0:T(8,128)(2,1)} %collective-permute-done.g_ref.b_ref.c_ref, bf16[384,2560]{1,0:T(8,128)(2,1)} %collective-permute-done.g_ref.b_ref.c_ref, f32[32,512]{1,0:T(8,128)} %copy-done.12, ...), custom_call_target="tpu_custom_call" | custom-call | flops 4000000000 | bytes 4000000 | tf_op jit(solution)/shard_map/passed_grads/pallas_call | solution.py:470
  100.2 0.0 collective-permute-done.3
  100.2 5.9 %collective-permute-done.4 = bf16[384,1024]{1,0:T(8,128)(2,1)S(1)} collective-permute-done((bf16[384,1024]{1,0:T(8,128)(2,1)}, bf16[384,1024]{1,0:T(8,128)(2,1)S(1)}, u32[]{:S(2)}, u32[]{:S(2)}) %collective-permute-start.4) | collective-permute-done | bytes 786464 | tf_op jit(solution)/shard_map/ppermute | solution.py:356
  106.2 3.0 %maximum_bitcast_fusion = bf16[1,384,4096]{2,1,0:T(8,128)(2,1)} fusion(bf16[384,1024]{1,0:T(8,128)(2,1)S(1)} %collective-permute-done.4, bf16[384,1024]{1,0:T(8,128)(2,1)S(1)} %collective-permute-done.3, bf16[384,2048]{1,0:T(8,128)(2,1)} %passed_grads.1), kind=kLoop, calls=%fused_computation | loop fusion | flops 9437184 | bytes 6291456 | tf_op jit(solution)/shard_map/broadcast_in_dim | solution.py:498
  (1 shorter events, 0.0 us)
Async XLA Ops:
  3.6 87.2 %collective-permute-start = (bf16[384,2560]{1,0:T(8,128)(2,1)}, bf16[384,2560]{1,0:T(8,128)(2,1)}, u32[]{:S(2)}, u32[]{:S(2)}) collective-permute-start(bf16[384,2560]{1,0:T(8,128)(2,1)} %get-tuple-element.26), channel_id=1, source_target_pairs={{0,24},{8,0},{16,8},{24,16},{1,25},{9,1},{17,9},{25,17},{2,26},{10... | collective-permute-start | bytes 5898248 | tf_op jit(solution)/shard_map/ppermute | solution.py:356
  7.5 50.5 %copy-start.11 = (f32[32,512]{1,0:T(8,128)S(1)}, f32[32,512]{1,0:T(8,128)}, u32[]{:S(2)}) copy-start(f32[32,512]{1,0:T(8,128)} %get-tuple-element.27) | copy-start | bytes 196612
  7.5 51.6 %copy-start.9 = (f32[1,64]{1,0:T(1,128)S(1)}, f32[1,64]{1,0:T(1,128)}, u32[]{:S(2)}) copy-start(f32[1,64]{1,0:T(1,128)} %skip_ref.1) | copy-start | bytes 772
  57.0 33.7 %collective-permute-start.2 = (bf16[4,128,512]{2,1,0:T(8,128)(2,1)S(1)}, bf16[4,128,512]{2,1,0:T(8,128)(2,1)S(1)}, u32[]{:S(2)}, u32[]{:S(2)}) collective-permute-start(bf16[4,128,512]{2,1,0:T(8,128)(2,1)S(1)} %slice.3), channel_id=1, source_target_pairs={{0,24},{8,0},{16,8},{24,16},{1,25},{9,1},{17,9},{25,17},{2,26},{10... | collective-permute-start | bytes 1572872 | tf_op jit(solution)/shard_map/ppermute | solution.py:356
  58.0 32.7 %collective-permute-start.1 = (f32[32,512]{1,0:T(8,128)S(1)}, f32[32,512]{1,0:T(8,128)S(1)}, u32[]{:S(2)}, u32[]{:S(2)}) collective-permute-start(f32[32,512]{1,0:T(8,128)S(1)} %copy-done.11), channel_id=1, source_target_pairs={{0,24},{8,0},{16,8},{24,16},{1,25},{9,1},{17,9},{25,17},{2,26},{10... | collective-permute-start | bytes 196616 | tf_op jit(solution)/shard_map/ppermute | solution.py:356
  66.1 34.1 %collective-permute-start.3 = (bf16[384,1024]{1,0:T(8,128)(2,1)}, bf16[384,1024]{1,0:T(8,128)(2,1)S(1)}, u32[]{:S(2)}, u32[]{:S(2)}) collective-permute-start(bf16[384,1024]{1,0:T(8,128)(2,1)} %get-tuple-element.34), channel_id=1, source_target_pairs={{0,24},{8,0},{16,8},{24,16},{1,25},{9,1},{17,9},{25,17},{2,26},{10... | collective-permute-start | bytes 2359304 | tf_op jit(solution)/shard_map/ppermute | solution.py:356
  73.4 32.8 %collective-permute-start.4 = (bf16[384,1024]{1,0:T(8,128)(2,1)}, bf16[384,1024]{1,0:T(8,128)(2,1)S(1)}, u32[]{:S(2)}, u32[]{:S(2)}) collective-permute-start(bf16[384,1024]{1,0:T(8,128)(2,1)} %get-tuple-element.35), channel_id=1, source_target_pairs={{0,24},{8,0},{16,8},{24,16},{1,25},{9,1},{17,9},{25,17},{2,26},{10... | collective-permute-start | bytes 2359304 | tf_op jit(solution)/shard_map/ppermute | solution.py:356
  81.3 6.1 %copy-start = (bf16[384,128]{1,0:T(8,128)(2,1)S(1)}, bf16[384,128]{1,0:T(8,128)(2,1)}, u32[]{:S(2)}) copy-start(bf16[384,128]{1,0:T(8,128)(2,1)} %get-tuple-element.38) | copy-start | bytes 294916
  81.3 6.1 %copy-start.1 = (bf16[384,128]{1,0:T(8,128)(2,1)S(1)}, bf16[384,128]{1,0:T(8,128)(2,1)}, u32[]{:S(2)}) copy-start(bf16[384,128]{1,0:T(8,128)(2,1)} %get-tuple-element.42) | copy-start | bytes 294916
  81.3 6.1 %copy-start.2 = (bf16[384,128]{1,0:T(8,128)(2,1)S(1)}, bf16[384,128]{1,0:T(8,128)(2,1)}, u32[]{:S(2)}) copy-start(bf16[384,128]{1,0:T(8,128)(2,1)} %get-tuple-element.39) | copy-start | bytes 294916
  81.3 6.1 %copy-start.3 = (bf16[384,128]{1,0:T(8,128)(2,1)S(1)}, bf16[384,128]{1,0:T(8,128)(2,1)}, u32[]{:S(2)}) copy-start(bf16[384,128]{1,0:T(8,128)(2,1)} %get-tuple-element.43) | copy-start | bytes 294916
  81.3 6.1 %copy-start.4 = (bf16[384,128]{1,0:T(8,128)(2,1)S(1)}, bf16[384,128]{1,0:T(8,128)(2,1)}, u32[]{:S(2)}) copy-start(bf16[384,128]{1,0:T(8,128)(2,1)} %get-tuple-element.36) | copy-start | bytes 294916
  81.3 6.1 %copy-start.5 = (bf16[384,128]{1,0:T(8,128)(2,1)S(1)}, bf16[384,128]{1,0:T(8,128)(2,1)}, u32[]{:S(2)}) copy-start(bf16[384,128]{1,0:T(8,128)(2,1)} %get-tuple-element.40) | copy-start | bytes 294916
  81.3 8.0 %copy-start.6 = (f32[16,384]{1,0:T(8,128)S(1)}, f32[16,384]{1,0:T(8,128)}, u32[]{:S(2)}) copy-start(f32[16,384]{1,0:T(8,128)} %get-tuple-element.46) | copy-start | bytes 73732
  81.4 8.0 %copy-start.7 = (f32[16,384]{1,0:T(8,128)S(1)}, f32[16,384]{1,0:T(8,128)}, u32[]{:S(2)}) copy-start(f32[16,384]{1,0:T(8,128)} %get-tuple-element.47) | copy-start | bytes 73732
  81.4 8.0 %copy-start.8 = (f32[16,384]{1,0:T(8,128)S(1)}, f32[16,384]{1,0:T(8,128)}, u32[]{:S(2)}) copy-start(f32[16,384]{1,0:T(8,128)} %get-tuple-element.44) | copy-start | bytes 73732
  90.7 0.6 copy-start.12
  90.7 0.8 copy-start.10

commit v3 on v2

--- a/solution.py
+++ b/solution.py
@@ -15,6 +15,7 @@
 W = HPG * P_SIZE
 Q = 128
 PIECES = 8
+SKEW = 2
 RAW = 2
 LOG2E = 1.4426950408889634
 MESH = pl.DeviceIdType.MESH
@@ -58,7 +59,7 @@
     return sum(dot(lower, part, 1, 1) for part in split3(twice))
 
 
-def relay_kernel(n, halves, half, x_hbm, b_hbm, c_hbm, decay_hbm, g_hbm, ent_ref, adj_ref, gx_ref, db_ref, dc_ref, diff_ref,
+def relay_kernel(n, halves, half, x_hbm, b_hbm, c_hbm, decay_hbm, g_hbm, ent_ref, adj_ref, gx_ref, db_ref, dc_ref, diff_ref, first_adj_ref,
                  mixed_ref, row_ref, col_ref, xv, bv, cv, dv, gv, s_ref, a_ref, e_ref, fs, bs, small_sem, wide_sem, fsend, frecv, bsend, brecv):
     me = lax.axis_index("ctx")
     pipe = lax.axis_index("pipe")
@@ -111,24 +112,30 @@
             e_ref[group * halves + k] = start[length - 1 : length, cut]
 
     chunks = length // Q
-    col_ref[...] = jnp.zeros((Q, Q), F32)
-
-    def unit(group, c):
+    col_ref[...] = jnp.zeros(col_ref.shape, F32)
+    few = HPG // 2
+
+    def unit(group, c, part):
         square = (Q, Q)
         lower = ones_where(iota(square, 1) <= iota(square, 0))
         upper = ones_where(iota(square, 0) <= iota(square, 1))
         rows = pl.ds(pl.multiple_of(c * Q, Q), Q)
         lanes_n = pl.ds(pl.multiple_of(group * N, N), N)
-        decay = dv[pl.ds(pl.multiple_of(group * HPG, HPG), HPG), rows] * LOG2E
-        cqt = columns_cumulative(decay, lower)
-        cq = sum(dot(part, upper) for part in split3(decay))
+        pieces = split3(dv[pl.ds(pl.multiple_of(group * HPG + part * few, few), few), rows] * LOG2E)
+        cqt = sum(dot(lower, piece, 1, 1) for piece in pieces)
+        cq = sum(dot(piece, upper) for piece in pieces)
         bc = bv[rows, lanes_n]
         cc = cv[rows, lanes_n]
         valid = iota(square, 1) >= iota(square, 0)
         inner = jnp.where(valid, dot(bc, cc, 1, 1), 0.0)
         low_lane = iota(square, 1) < P_SIZE
-        for pair in range(HPG // 2):
-            lanes = slice(pair * 128, (pair + 1) * 128)
+
+        @pl.when(part == 0)
+        def _():
+            mixed_ref[...] = jnp.zeros(square, F32)
+
+        for pair in range(few // 2):
+            lanes = pl.ds(pl.multiple_of(part * (W // 2) + pair * 128, 128), 128)
             xp = xv[group, rows, lanes]
             gp = gv[group, rows, lanes]
             zero = jnp.zeros_like(gp)
@@ -143,17 +150,18 @@
                 mixed = kp if mixed is None else mixed + kp
                 inners.append((kernel * inner).astype(BF16))
                 joint = kp * inner
-                row_ref[h : h + 1, :] = jnp.sum(joint, axis=0, keepdims=True)
-                col_ref[:, h : h + 1] = jnp.sum(joint, axis=1, keepdims=True)
-            if pair == 0:
-                mixed_ref[...] = mixed
-            else:
-                mixed_ref[...] += mixed
+                row_ref[part, h : h + 1, :] = jnp.sum(joint, axis=0, keepdims=True)
+                col_ref[part, :, h : h + 1] = jnp.sum(joint, axis=1, keepdims=True)
+            mixed_ref[...] += mixed
             gx_ref[group, rows, lanes] = dot(jnp.concatenate(inners, axis=1), gm).astype(BF16)
-        mixed_t = jnp.where(valid, mixed_ref[...], 0.0)
-        db_ref[rows, lanes_n] = dot(mixed_t.astype(BF16), cc)
-        dc_ref[rows, lanes_n] = dot(mixed_t.T.astype(BF16), bc)
-        diff_ref[group * chunks + c] = row_ref[...] - col_ref[...].T[:HPG, :]
+
+        @pl.when(part == 1)
+        def _():
+            mixed_t = jnp.where(valid, mixed_ref[...], 0.0)
+            db_ref[rows, lanes_n] = dot(mixed_t.astype(BF16), cc)
+            dc_ref[rows, lanes_n] = dot(mixed_t.T.astype(BF16), bc)
+            for at in range(2):
+                diff_ref[group * chunks + c, at * few : (at + 1) * few, :] = row_ref[at] - col_ref[at].T[:few, :]
 
     def forward(k):
         return pltpu.make_async_remote_copy(
@@ -180,8 +188,8 @@
             make(k).start()
 
     def step(t, carry):
-        kf = t - me
-        kb = t - (n - 1 - me)
+        kf = t - SKEW * me
+        kb = t - SKEW * (n - 1 - me)
 
         @pl.when(jnp.logical_and(lax.rem(t, halves) == 0, t < PIECES))
         def _():
@@ -199,13 +207,15 @@
         def _():
             advance(kb, n - 1 - me, backward, adj_ref, a_ref, bs)
 
-        @pl.when(t < G * chunks)
-        def _():
-            unit(lax.div(t, chunks), lax.rem(t, chunks))
+        @pl.when(t < 2 * G * chunks)
+        def _():
+            unit(lax.div(t, 2 * chunks), lax.rem(lax.div(t, 2), chunks), lax.rem(t, 2))
 
         return carry
 
-    lax.fori_loop(0, max(n + PIECES - 1, G * chunks), step, 0)
+    lax.fori_loop(0, max(SKEW * (n - 1) + PIECES, 2 * G * chunks), step, 0)
+
+    first_adj_ref[...] = adj_ref[: RAW * halves]
 
     @pl.when(me < n - 1)
     def _():
@@ -218,10 +228,14 @@
             backward(k).wait_send()
 
 
-def group_kernel(with_x, x_ref, b_ref, c_ref, decay_ref, g_ref, skip_ref, ent_ref, adj_ref,
+def group_kernel(first, with_x, carried, x_ref, b_ref, c_ref, decay_ref, g_ref, skip_ref, ent_ref, adj_ref,
                  near_db_ref, near_dc_ref, diff_ref, *refs):
+    refs = refs[carried:]
     if with_x:
         near_gx_ref, gx_ref, *refs = refs
+        group = first + pl.program_id(0)
+        own = iota((HPG, H), 1) == iota((HPG, H), 0) + group * HPG
+        column = jnp.sum(jnp.where(own, skip_ref[...], 0.0), axis=1, keepdims=True)
     db_ref, dc_ref, gd_ref, es_ref, ds_ref = refs
     chunks = x_ref.shape[0] // Q
     square = (Q, Q)
@@ -230,6 +244,8 @@
     heads = ones_where(iota((HPG, W), 0) == iota((HPG, W), 1) // P_SIZE)
     wide = heads.astype(F32)
     half = ent_ref.shape[2]
+    if with_x:
+        skip = jnp.sum(wide * column, axis=0, keepdims=True)
 
     for k in range(W // half):
         es_ref[0, :, k * half : (k + 1) * half] = ent_ref[k]
@@ -256,7 +272,7 @@
         edge = dot(b_ref[rows, :], adj)
         if with_x:
             gx_ref[rows, :] = (
-                near_gx_ref[0, rows, :].astype(F32) + ends[c] * edge + skip_ref[...] * g_ref[rows, :].astype(F32)
+                near_gx_ref[0, rows, :].astype(F32) + ends[c] * edge + skip * g_ref[rows, :].astype(F32)
             ).astype(BF16)
         db_ref[rows, :] = (near_db_ref[rows, :] + dot(xws[c], adj, 1, 1)).astype(BF16)
         dc_ref[rows, :] = (near_dc_ref[rows, :] + dot(gws[c], ent, 1, 1)).astype(BF16)
@@ -272,6 +288,10 @@
         grads = diff_ref[c] + terms
         grads = grads + jnp.where(iota((HPG, Q), 1) == Q - 1, last, 0.0)
         gd_ref[:, rows] = sum(dot(part, lower) for part in split3(grads))
+
+
+def place_kernel(piece_ref, whole_ref, out_ref):
+    out_ref[...] = piece_ref[...]
 
 
 def pack_kernel(heads, g_ref, b_ref, c_ref, decay_ref, skip_ref, raw_ref, out_ref):
@@ -348,7 +368,6 @@
     n = lax.axis_size("ctx")
     half = G * W // PIECES
     halves = W // half
-    skip = jnp.repeat(skip_gain, P_SIZE, axis=1)
     devices = lax.axis_size("pipe")
     route = [(source, (source - 1) % devices) for source in range(devices)]
 
@@ -383,10 +402,10 @@
     raw_decay = send(raw_decay)
 
     states = jax.ShapeDtypeStruct((PIECES, N, half), BF16)
-    entering, adjoint, near_gx, near_db, near_dc, diff = pl.pallas_call(
+    entering, adjoint, near_gx, near_db, near_dc, diff, first_adjoint = pl.pallas_call(
         functools.partial(relay_kernel, n, halves, half),
         in_specs=[away] * 5,
-        out_specs=[whole] * 6,
+        out_specs=[whole] * 7,
         out_shape=[
             states,
             states,
@@ -394,11 +413,12 @@
             jax.ShapeDtypeStruct((length, G * N), F32),
             jax.ShapeDtypeStruct((length, G * N), F32),
             jax.ShapeDtypeStruct((G * chunks, HPG, Q), F32),
+            jax.ShapeDtypeStruct((RAW * halves, N, half), BF16),
         ],
         scratch_shapes=[
             pltpu.VMEM((Q, Q), F32),
-            pltpu.VMEM((HPG, Q), F32),
-            pltpu.VMEM((Q, Q), F32),
+            pltpu.VMEM((2, HPG // 2, Q), F32),
+            pltpu.VMEM((2, Q, Q), F32),
             pltpu.VMEM((G, length, W), BF16),
             pltpu.VMEM((length, G * N), BF16),
             pltpu.VMEM((length, G * N), BF16),
@@ -416,58 +436,60 @@
         cost_estimate=pl.CostEstimate(flops=30_000_000_000, bytes_accessed=8_000_000, transcendentals=1_000_000),
         name="relay",
     )(x, b, c, decay, g)
-    raw_adjoint = send(adjoint[: RAW * halves])
-
-    def own_group(group, with_x):
-        pick = lambda i: (0, group)
-        rows = lambda i: (group, 0)
-        pieces = pl.BlockSpec((halves, N, half), lambda i: (group, 0, 0))
-        flat = lambda i: (0, 0)
+    raw_adjoint = send(first_adjoint)
+
+    def own_groups(first, count, with_x, carry):
+        pick = lambda i: (0, first + i)
+        rows = lambda i: (first + i, 0)
+        deep = lambda i: (first + i, 0, 0)
+        pieces = pl.BlockSpec((halves, N, half), deep)
         out_specs = [
-            pl.BlockSpec((length, W), flat),
-            pl.BlockSpec((length, N), flat),
-            pl.BlockSpec((length, N), flat),
-            pl.BlockSpec((HPG, length), flat),
+            pl.BlockSpec((length, W), lambda i: (0, i)),
+            pl.BlockSpec((length, N), pick),
+            pl.BlockSpec((length, N), pick),
+            pl.BlockSpec((HPG, length), rows),
         ]
         out_shape = [
-            jax.ShapeDtypeStruct((length, W), BF16),
-            jax.ShapeDtypeStruct((length, N), BF16),
-            jax.ShapeDtypeStruct((length, N), BF16),
-            jax.ShapeDtypeStruct((HPG, length), F32),
+            jax.ShapeDtypeStruct((length, count * W), BF16),
+            jax.ShapeDtypeStruct((length, G * N), BF16),
+            jax.ShapeDtypeStruct((length, G * N), BF16),
+            jax.ShapeDtypeStruct((H, length), F32),
         ]
-        first = 0 if with_x else 1
+        skipped = 0 if with_x else 1
+        carried = len(carry)
+        wide_in = [near_gx] if with_x else []
         return pl.pallas_call(
-            functools.partial(group_kernel, with_x),
-            grid=(1,),
+            functools.partial(group_kernel, first, with_x, carried),
+            grid=(count,),
             in_specs=[
                 pl.BlockSpec((length, W), pick),
                 pl.BlockSpec((length, N), pick),
                 pl.BlockSpec((length, N), pick),
                 pl.BlockSpec((HPG, length), rows),
                 pl.BlockSpec((length, W), pick),
-                pl.BlockSpec((1, W), pick),
+                pl.BlockSpec((1, H), lambda i: (0, 0)),
                 pieces,
                 pieces,
                 pl.BlockSpec((length, N), pick),
                 pl.BlockSpec((length, N), pick),
-                pl.BlockSpec((chunks, HPG, Q), lambda i: (group, 0, 0)),
-            ] + [pl.BlockSpec((1, length, W), lambda i: (group, 0, 0))] * with_x,
-            out_specs=out_specs[first:],
-            out_shape=out_shape[first:],
+                pl.BlockSpec((chunks, HPG, Q), deep),
+            ] + [away] * carried + [pl.BlockSpec((1, length, W), deep)] * len(wide_in),
+            out_specs=out_specs[skipped:],
+            out_shape=out_shape[skipped:],
+            input_output_aliases={11 + at: at + 1 - skipped for at in range(carried)},
             scratch_shapes=[pltpu.VMEM((chunks, N, W), BF16), pltpu.VMEM((chunks, N, W), BF16)],
             compiler_params=pltpu.CompilerParams(vmem_limit_bytes=60 << 20),
             cost_estimate=pl.CostEstimate(flops=3_000_000_000, bytes_accessed=4_000_000, transcendentals=1_000_000),
             name="group_grads",
-        )(x, b, c, decay, g, skip, entering, adjoint, near_db, near_dc, diff, *[near_gx][: int(with_x)])
+        )(x, b, c, decay, g, skip_gain, entering, adjoint, near_db, near_dc, diff, *carry, *wide_in)
 
     sent = {}
-    rest = {}
-    for group in list(range(RAW, G)) + list(range(RAW)):
-        out = own_group(group, group >= RAW)
-        if group >= RAW:
-            sent[group] = send(out[0])
-        rest[group] = out[-3:]
-    passed_first = pl.pallas_call(
+    carry = ()
+    for group in range(RAW, G):
+        grads, *carry = own_groups(group, 1, True, carry)
+        sent[group] = send(grads)
+    grad_b, grad_c, grad_decay = own_groups(0, RAW, False, carry)
+    grad_x = pl.pallas_call(
         passed_kernel,
         grid=(RAW,),
         in_specs=[
@@ -478,7 +500,7 @@
             pl.BlockSpec((halves, N, half), lambda i: (i, 0, 0)),
         ],
         out_specs=pl.BlockSpec((length, W), lambda i: (0, i)),
-        out_shape=jax.ShapeDtypeStruct((length, RAW * W), BF16),
+        out_shape=jax.ShapeDtypeStruct((length, G * W), BF16),
         scratch_shapes=[
             pltpu.VMEM((length, W), BF16),
             pltpu.VMEM((length, W), F32),
@@ -491,10 +513,17 @@
         cost_estimate=pl.CostEstimate(flops=4_000_000_000, bytes_accessed=4_000_000, transcendentals=1_000_000),
         name="passed_grads",
     )(raw, raw, raw, raw_decay, raw_adjoint)
-    grad_x = jnp.concatenate([passed_first] + [sent[group] for group in range(RAW, G)], axis=1)
-    grad_b = jnp.concatenate([rest[group][0] for group in range(G)], axis=1)
-    grad_c = jnp.concatenate([rest[group][1] for group in range(G)], axis=1)
-    grad_decay = jnp.concatenate([rest[group][2] for group in range(G)], axis=0)
+    for group in range(RAW, G):
+        grad_x = pl.pallas_call(
+            place_kernel,
+            grid=(1,),
+            in_specs=[pl.BlockSpec((length, W), lambda i: (0, 0)), away],
+            out_specs=pl.BlockSpec((length, W), lambda i, group=group: (0, group)),
+            out_shape=jax.ShapeDtypeStruct((length, G * W), BF16),
+            input_output_aliases={1: 0},
+            compiler_params=pltpu.CompilerParams(vmem_limit_bytes=60 << 20),
+            name="place_grads",
+        )(sent[group], grad_x)
     return grad_x[None], grad_b[None], grad_c[None], grad_decay[None]
 
 

time: 110 us -> 117 us (1.064)
  waiting for transfers between devices: 5.93 us -> 22.1 us
  other arithmetic: 6.25 us -> 0 us
  Pallas kernels: 84.6 us -> 81.4 us
  local copies, waits for them, and re-layouts: 2.68 us -> 3.94 us
    ppermute x5, waiting for transfers between devices: 5.93 us -> 22.1 us  [send(): return lax.ppermute(value, 'pipe', route)]
    broadcast_in_dim x3 -> x0, other arithmetic: 6.25 us -> none  [local(): return (grad_x[None], grad_b[None], grad_c[None], grad_decay[None])]
    pallas_call x1, Pallas kernels: 48.4 us -> 42.6 us  [local(): pl.pallas_call(functools.partial(relay_kernel, n, halves, half), in_specs...]
    unnamed x26 -> x10, local copies, waits for them, and re-layouts: 0.84 us -> 3.94 us
    pallas_call x4 -> x5, Pallas kernels: 24.5 us -> 27.1 us  [the longest x3 23 us: own_groups(): pl.pallas_call(functools.partial(group_kernel, first, with_x, carried), g...]
  transfers between devices with their start and end apart: 5 -> 5, of which waited for: 1 -> 1; matrix products, arithmetic and copies ran while one was open for 5% -> 0% of each run, Pallas kernels for 75% -> 65%
where the time goes in v3:
time: 117 us
  Pallas kernels  81.4 us (70%)
  waiting for transfers between devices  22.1 us (19%)
  starting transfers between devices  8.9 us (8%)
  local copies, waits for them, and re-layouts  3.94 us (3%)
    pallas_call x1, Pallas kernels, local(): pl.pallas_call(functools.partial(relay_kernel, n, halves, half), in_specs...  42.6 us
    pallas_call x3, Pallas kernels, own_groups(): pl.pallas_call(functools.partial(group_kernel, first, with_x, carried), g...  23 us
    ppermute x5, waiting for transfers between devices, send(): return lax.ppermute(value, 'pipe', route)  22.1 us
    ppermute x5, starting transfers between devices, send(): return lax.ppermute(value, 'pipe', route)  8.9 us
    pallas_call x1, Pallas kernels, local(): pl.pallas_call(passed_kernel, grid=(RAW,), in_specs=[pl.BlockSpec((length...  8.64 us
    pallas_call x2, Pallas kernels, local(): pl.pallas_call(place_kernel, grid=(1,), in_specs=[pl.BlockSpec((length, W...  4.12 us
    unnamed x10, local copies, waits for them, and re-layouts  3.94 us
    pallas_call x1, Pallas kernels, local(): pl.pallas_call(functools.partial(pack_kernel, heads), grid=(1,), in_specs...  2.97 us
  transfers between devices with their start and end apart: 5, of which 1 were waited for; matrix products, arithmetic and copies ran while one was open for 0% of the time, Pallas kernels for 65%

profile of v3, /device:TPU:0, one launch (start us, length us, event | category | flops | bytes accessed | tf_op | source)
XLA Modules:
  0.0 117.0 jit_solution(17120963148296093014)
XLA Ops:
  0.6 3.0 %pack_raw.1 = (bf16[384,2560]{1,0:T(8,128)(2,1)}, f32[32,512]{1,0:T(8,128)}) custom-call(bf16[384,4096]{1,0:T(8,128)(2,1)} %bitcast.9, bf16[384,512]{1,0:T(8,128)(2,1)} %bitcast.19, bf16[384,512]{1,0:T(8,128)(2,1)} %bitcast.24, f32[64,384]{1,0:T(8,128)} %bitcast.29, f32[1,64]{1,0:T(1,128)} %skip_ref.7), custom_call_target="tpu_custom_call" | custom-call | tf_op jit(solution)/shard_map/pack_raw/pallas_call | solution.py:380
  3.6 3.9 %collective-permute-start.2 = (bf16[384,2560]{1,0:T(8,128)(2,1)}, bf16[384,2560]{1,0:T(8,128)(2,1)S(1)}, u32[]{:S(2)}, u32[]{:S(2)}) collective-permute-start(bf16[384,2560]{1,0:T(8,128)(2,1)} %get-tuple-element.35), channel_id=1, source_target_pairs={{0,24},{8,0},{16,8},{24,16},{1,25},{9,1},{17,9},{25,17},{2,26},{10... | collective-permute-start | bytes 5898248 | tf_op jit(solution)/shard_map/ppermute | solution.py:375
  7.5 42.6 %relay.1 = (bf16[8,128,512]{2,1,0:T(8,128)(2,1)}, bf16[8,128,512]{2,1,0:T(8,128)(2,1)}, bf16[4,384,1024]{2,1,0:T(8,128)(2,1)}, f32[384,512]{1,0:T(8,128)}, f32[3...) custom-call(bf16[384,4096]{1,0:T(8,128)(2,1)} %bitcast.14, bf16[384,512]{1,0:T(8,128)(2,1)} %bitcast.20, ...), custom_call_target="tpu_custom_call" | custom-call | flops 30000001024 | bytes 8000000 | tf_op jit(solution)/shard_map/relay/pallas_call | solution.py:405
  50.1 0.6 collective-permute-start.4
  50.7 6.7 %group_grads.3 = (bf16[384,1024]{1,0:T(8,128)(2,1)}, bf16[384,512]{1,0:T(8,128)(2,1)}, bf16[384,512]{1,0:T(8,128)(2,1)}, f32[64,384]{1,0:T(8,128)}) custom-call(bf16[384,4096]{1,0:T(8,128)(2,1)} %bitcast.15, bf16[384,512]{1,0:T(8,128)(2,1)} %bitcast.21, bf16[384,512]{1,0:T(8,128)(2,1)} %bitcast.26, f32[64,384]{1,0:T(8,128)} %bitcast.31, ...), custom_call_target="tpu_custom_call" | custom-call | flops 3000000000 | bytes 4000000 | tf_op jit(solution)/shard_map/group_grads/pallas_call | solution.py:461
  57.4 1.4 %collective-permute-start.1 = (bf16[384,1024]{1,0:T(8,128)(2,1)}, bf16[384,1024]{1,0:T(8,128)(2,1)S(1)}, u32[]{:S(2)}, u32[]{:S(2)}) collective-permute-start(bf16[384,1024]{1,0:T(8,128)(2,1)} %get-tuple-element.34), channel_id=1, source_target_pairs={{0,24},{8,0},{16,8},{24,16},{1,25},{9,1},{17,9},{25,17},{2,26},{10... | collective-permute-start | bytes 2359304 | tf_op jit(solution)/shard_map/ppermute | solution.py:375
  58.8 0.0 copy-start.4
  58.8 6.7 %group_grads.4 = (bf16[384,1024]{1,0:T(8,128)(2,1)}, bf16[384,512]{1,0:T(8,128)(2,1)}, bf16[384,512]{1,0:T(8,128)(2,1)}, f32[64,384]{1,0:T(8,128)}) custom-call(bf16[384,4096]{1,0:T(8,128)(2,1)} %bitcast.16, bf16[384,512]{1,0:T(8,128)(2,1)} %bitcast.22, bf16[384,512]{1,0:T(8,128)(2,1)} %bitcast.27, ...), custom_call_target="tpu_custom_call", output_to_operand_aliasing={{1}: (11, {}), {2}: (12, {}), {3}: (13, {})} | custom-call | flops 3000000000 | bytes 4000000 | tf_op jit(solution)/shard_map/group_grads/pallas_call | solution.py:461
  65.5 0.5 collective-permute-start
  66.1 0.0 copy-done.4
  66.1 2.4 %collective-permute-start.3 = (f32[32,512]{1,0:T(8,128)S(1)}, f32[32,512]{1,0:T(8,128)}, u32[]{:S(2)}, u32[]{:S(2)}) collective-permute-start(f32[32,512]{1,0:T(8,128)S(1)} %copy-done.4), channel_id=1, source_target_pairs={{0,24},{8,0},{16,8},{24,16},{1,25},{9,1},{17,9},{25,17},{2,26},{10... | collective-permute-start | bytes 196616 | tf_op jit(solution)/shard_map/ppermute | solution.py:375
  68.5 9.7 %group_grads.5 = (bf16[384,512]{1,0:T(8,128)(2,1)}, bf16[384,512]{1,0:T(8,128)(2,1)}, f32[64,384]{1,0:T(8,128)}) custom-call(bf16[384,4096]{1,0:T(8,128)(2,1)} %bitcast.17, bf16[384,512]{1,0:T(8,128)(2,1)} %bitcast.23, bf16[384,512]{1,0:T(8,128)(2,1)} %bitcast.28, f32[64,384]{1,0:T(8,128)} %bitcast.33, ...), custom_call_target="tpu_custom_call", output_to_operand_aliasing={{0}: (11, {}), {1}: (12, {}), {2}: (13, {})} | custom-call | flops 3000000000 | bytes 4000000 | tf_op jit(solution)/shard_map/group_grads/pallas_call | solution.py:461
  78.2 22.1 %collective-permute-done.3.decay_ref = f32[32,512]{1,0:T(8,128)} collective-permute-done((f32[32,512]{1,0:T(8,128)S(1)}, f32[32,512]{1,0:T(8,128)}, u32[]{:S(2)}, u32[]{:S(2)}) %collective-permute-start.3) | collective-permute-done | bytes 65568 | tf_op jit(solution)/shard_map/ppermute | solution.py:375
  100.2 0.0 collective-permute-done.4.adj_ref
  100.2 0.0 copy-start.3
  100.3 0.0 collective-permute-done.2.g_ref.b_ref.c_ref
  100.3 0.8 copy-done.3
  101.1 0.0 copy-start.2
  101.1 1.3 %copy-done.2 = bf16[384,2560]{1,0:T(8,128)(2,1)} copy-done((bf16[384,2560]{1,0:T(8,128)(2,1)}, bf16[384,2560]{1,0:T(8,128)(2,1)S(1)}, u32[]{:S(2)}) %copy-start.2) | copy-done | bytes 1966104
  102.4 8.6 %passed_grads.1.whole_ref = bf16[384,4096]{1,0:T(8,128)(2,1)} custom-call(bf16[384,2560]{1,0:T(8,128)(2,1)} %copy-done.2, bf16[384,2560]{1,0:T(8,128)(2,1)} %copy-done.2, bf16[384,2560]{1,0:T(8,128)(2,1)} %copy-done.2, f32[32,512]{1,0:T(8,128)} %collective-permute-done.3.decay_ref, bf16[4,128,512]{2,1,0:T(8,128)(2,1)} %copy-done.3), custom_call_target="tpu_custom_call" | custom-call | flops 4000000000 | bytes 4000000 | tf_op jit(solution)/shard_map/passed_grads/pallas_call | solution.py:492
  111.0 0.0 collective-permute-done.1.piece_ref
  111.0 0.0 copy-start
  111.0 0.9 copy-done
  111.9 2.1 %place_grads.2.whole_ref = bf16[384,4096]{1,0:T(8,128)(2,1)} custom-call(bf16[384,1024]{1,0:T(8,128)(2,1)} %copy-done, bf16[384,4096]{1,0:T(8,128)(2,1)} %passed_grads.1.whole_ref), custom_call_target="tpu_custom_call", output_to_operand_aliasing={{}: (1, {})} | custom-call | tf_op jit(solution)/shard_map/place_grads/pallas_call | solution.py:517
  114.0 0.0 collective-permute-done.piece_ref
  114.0 0.0 copy-start.1
  114.0 0.9 copy-done.1
  114.9 2.1 %place_grads.3 = bf16[384,4096]{1,0:T(8,128)(2,1)} custom-call(bf16[384,1024]{1,0:T(8,128)(2,1)} %copy-done.1, bf16[384,4096]{1,0:T(8,128)(2,1)} %place_grads.2.whole_ref), custom_call_target="tpu_custom_call", output_to_operand_aliasing={{}: (1, {})} | custom-call | tf_op jit(solution)/shard_map/place_grads/pallas_call | solution.py:517
Async XLA Ops:
  3.6 96.7 %collective-permute-start.2 = (bf16[384,2560]{1,0:T(8,128)(2,1)}, bf16[384,2560]{1,0:T(8,128)(2,1)S(1)}, u32[]{:S(2)}, u32[]{:S(2)}) collective-permute-start(bf16[384,2560]{1,0:T(8,128)(2,1)} %get-tuple-element.35), channel_id=1, source_target_pairs={{0,24},{8,0},{16,8},{24,16},{1,25},{9,1},{17,9},{25,17},{2,26},{10... | collective-permute-start | bytes 5898248 | tf_op jit(solution)/shard_map/ppermute | solution.py:375
  50.1 50.1 %collective-permute-start.4 = (bf16[4,128,512]{2,1,0:T(8,128)(2,1)}, bf16[4,128,512]{2,1,0:T(8,128)(2,1)S(1)}, u32[]{:S(2)}, u32[]{:S(2)}) collective-permute-start(bf16[4,128,512]{2,1,0:T(8,128)(2,1)} %get-tuple-element.37), channel_id=1, source_target_pairs={{0,24},{8,0},{16,8},{24,16},{1,25},{9,1},{17,9},{25,17},{2,26},{10... | collective-permute-start | bytes 1572872 | tf_op jit(solution)/shard_map/ppermute | solution.py:375
  57.4 53.6 %collective-permute-start.1 = (bf16[384,1024]{1,0:T(8,128)(2,1)}, bf16[384,1024]{1,0:T(8,128)(2,1)S(1)}, u32[]{:S(2)}, u32[]{:S(2)}) collective-permute-start(bf16[384,1024]{1,0:T(8,128)(2,1)} %get-tuple-element.34), channel_id=1, source_target_pairs={{0,24},{8,0},{16,8},{24,16},{1,25},{9,1},{17,9},{25,17},{2,26},{10... | collective-permute-start | bytes 2359304 | tf_op jit(solution)/shard_map/ppermute | solution.py:375
  58.8 7.2 %copy-start.4 = (f32[32,512]{1,0:T(8,128)S(1)}, f32[32,512]{1,0:T(8,128)}, u32[]{:S(2)}) copy-start(f32[32,512]{1,0:T(8,128)} %get-tuple-element.36) | copy-start | bytes 196612
  65.5 48.4 %collective-permute-start = (bf16[384,1024]{1,0:T(8,128)(2,1)}, bf16[384,1024]{1,0:T(8,128)(2,1)S(1)}, u32[]{:S(2)}, u32[]{:S(2)}) collective-permute-start(bf16[384,1024]{1,0:T(8,128)(2,1)} %get-tuple-element.33), channel_id=1, source_target_pairs={{0,24},{8,0},{16,8},{24,16},{1,25},{9,1},{17,9},{25,17},{2,26},{10... | collective-permute-start | bytes 2359304 | tf_op jit(solution)/shard_map/ppermute | solution.py:375
  66.1 34.2 %collective-permute-start.3 = (f32[32,512]{1,0:T(8,128)S(1)}, f32[32,512]{1,0:T(8,128)}, u32[]{:S(2)}, u32[]{:S(2)}) collective-permute-start(f32[32,512]{1,0:T(8,128)S(1)} %copy-done.4), channel_id=1, source_target_pairs={{0,24},{8,0},{16,8},{24,16},{1,25},{9,1},{17,9},{25,17},{2,26},{10... | collective-permute-start | bytes 196616 | tf_op jit(solution)/shard_map/ppermute | solution.py:375
  100.2 0.8 copy-start.3
  101.1 1.3 %copy-start.2 = (bf16[384,2560]{1,0:T(8,128)(2,1)}, bf16[384,2560]{1,0:T(8,128)(2,1)S(1)}, u32[]{:S(2)}) copy-start(bf16[384,2560]{1,0:T(8,128)(2,1)S(1)} %collective-permute-done.2.g_ref.b_ref.c_ref) | copy-start | bytes 5898244
  111.0 0.9 copy-start
  114.0 0.9 copy-start.1

commit v4 on v3

--- a/solution.py
+++ b/solution.py
@@ -294,19 +294,23 @@
     out_ref[...] = piece_ref[...]
 
 
-def pack_kernel(heads, g_ref, b_ref, c_ref, decay_ref, skip_ref, raw_ref, out_ref):
+def pack_kernel(heads, g_ref, b_ref, c_ref, decay_ref, skip_ref, raw_ref):
     g_lanes, b_lanes = heads * P_SIZE, heads // HPG * N
+    last = g_lanes + 2 * b_lanes
     raw_ref[:, :g_lanes] = g_ref[...]
     raw_ref[:, g_lanes : g_lanes + b_lanes] = b_ref[...]
-    raw_ref[:, g_lanes + b_lanes :] = c_ref[...]
-    length = decay_ref.shape[1]
-    out_ref[:, :length] = decay_ref[...]
+    raw_ref[:, g_lanes + b_lanes : last] = c_ref[...]
+    chunks = decay_ref.shape[1] // Q
     own = iota((heads, H), 0) == iota((heads, H), 1)
     column = jnp.sum(jnp.where(own, skip_ref[...], 0.0), axis=1, keepdims=True)
-    out_ref[:, length:] = jnp.broadcast_to(column, (heads, 128))
-
-
-def passed_kernel(g_ref, b_ref, c_ref, decay_ref, adj_ref, gx_ref, gw_ref, end_ref, ds_ref, edge_ref, cq_ref, cqt_ref):
+    blocks = [decay_ref[:, c * Q : (c + 1) * Q] for c in range(chunks)] + [jnp.broadcast_to(column, (heads, Q))]
+    for at, block in enumerate(blocks):
+        for part, piece in enumerate(split3(block)):
+            row = (at * 3 + part) * heads
+            raw_ref[row : row + heads, last:] = piece
+
+
+def passed_kernel(heads, g_ref, b_ref, c_ref, scalars_ref, adj_ref, gx_ref, gw_ref, end_ref, ds_ref, edge_ref, cq_ref, cqt_ref):
     length = g_ref.shape[0]
     chunks = length // Q
     square = (Q, Q)
@@ -317,11 +321,19 @@
     for k in range(W // half):
         ds_ref[chunks - 1, :, k * half : (k + 1) * half] = adj_ref[k]
     wide = ones_where(iota((HPG, W), 0) == iota((HPG, W), 1) // P_SIZE).astype(F32)
-    skip = jnp.sum(wide * decay_ref[:, length : length + 1], axis=0, keepdims=True)
+    own = pl.program_id(0) * HPG
+
+    def scalars(at):
+        parts = [
+            scalars_ref[pl.ds(pl.multiple_of((at * 3 + part) * heads + own, HPG), HPG), :].astype(F32) for part in range(3)
+        ]
+        return parts[0] + parts[1] + parts[2]
+
+    skip = jnp.sum(wide * scalars(chunks)[:, :1], axis=0, keepdims=True)
     keep = []
     for c in range(chunks):
         rows = slice(c * Q, (c + 1) * Q)
-        decay = decay_ref[:, rows] * LOG2E
+        decay = scalars(c) * LOG2E
         cum = columns_cumulative(decay, lower)
         cqt_ref[c] = cum
         cq_ref[c] = sum(dot(part, upper) for part in split3(decay))
@@ -377,7 +389,8 @@
     heads = RAW * HPG
     whole = pl.BlockSpec(memory_space=pltpu.VMEM)
     away = pl.BlockSpec(memory_space=pl.ANY)
-    raw, raw_decay = pl.pallas_call(
+    raw_lanes = heads * P_SIZE + 2 * RAW * N + Q
+    raw = pl.pallas_call(
         functools.partial(pack_kernel, heads),
         grid=(1,),
         in_specs=[
@@ -387,19 +400,12 @@
             pl.BlockSpec((heads, length), lambda i: (0, 0)),
             pl.BlockSpec((1, H), lambda i: (0, 0)),
         ],
-        out_specs=[
-            pl.BlockSpec((length, heads * P_SIZE + 2 * RAW * N), lambda i: (0, 0)),
-            pl.BlockSpec((heads, length + 128), lambda i: (0, 0)),
-        ],
-        out_shape=[
-            jax.ShapeDtypeStruct((length, heads * P_SIZE + 2 * RAW * N), BF16),
-            jax.ShapeDtypeStruct((heads, length + 128), F32),
-        ],
+        out_specs=pl.BlockSpec((length, raw_lanes), lambda i: (0, 0)),
+        out_shape=jax.ShapeDtypeStruct((length, raw_lanes), BF16),
         compiler_params=pltpu.CompilerParams(vmem_limit_bytes=60 << 20),
         name="pack_raw",
     )(g, b, c, decay, skip_gain)
     raw = send(raw)
-    raw_decay = send(raw_decay)
 
     states = jax.ShapeDtypeStruct((PIECES, N, half), BF16)
     entering, adjoint, near_gx, near_db, near_dc, diff, first_adjoint = pl.pallas_call(
@@ -479,7 +485,7 @@
             input_output_aliases={11 + at: at + 1 - skipped for at in range(carried)},
             scratch_shapes=[pltpu.VMEM((chunks, N, W), BF16), pltpu.VMEM((chunks, N, W), BF16)],
             compiler_params=pltpu.CompilerParams(vmem_limit_bytes=60 << 20),
-            cost_estimate=pl.CostEstimate(flops=3_000_000_000, bytes_accessed=4_000_000, transcendentals=1_000_000),
+            cost_estimate=pl.CostEstimate(flops=300_000_000, bytes_accessed=400_000, transcendentals=1_000_000),
             name="group_grads",
         )(x, b, c, decay, g, skip_gain, entering, adjoint, near_db, near_dc, diff, *carry, *wide_in)
 
@@ -490,13 +496,13 @@
         sent[group] = send(grads)
     grad_b, grad_c, grad_decay = own_groups(0, RAW, False, carry)
     grad_x = pl.pallas_call(
-        passed_kernel,
+        functools.partial(passed_kernel, heads),
         grid=(RAW,),
         in_specs=[
             pl.BlockSpec((length, W), lambda i: (0, i)),
             pl.BlockSpec((length, N), lambda i: (0, RAW * (W // N) + i)),
             pl.BlockSpec((length, N), lambda i: (0, RAW * (W // N) + RAW + i)),
-            pl.BlockSpec((HPG, length + 128), lambda i: (i, 0)),
+            pl.BlockSpec((length, Q), lambda i: (0, raw_lanes // Q - 1)),
             pl.BlockSpec((halves, N, half), lambda i: (i, 0, 0)),
         ],
         out_specs=pl.BlockSpec((length, W), lambda i: (0, i)),
@@ -509,10 +515,10 @@
             pltpu.VMEM((chunks, HPG, Q), F32),
             pltpu.VMEM((chunks, Q, 2 * HPG), F32),
         ],
-        compiler_params=pltpu.CompilerParams(vmem_limit_bytes=60 << 20),
-        cost_estimate=pl.CostEstimate(flops=4_000_000_000, bytes_accessed=4_000_000, transcendentals=1_000_000),
+        compiler_params=pltpu.CompilerParams(vmem_limit_bytes=24 << 20),
+        cost_estimate=pl.CostEstimate(flops=4_000_000_000, bytes_accessed=400_000, transcendentals=1_000_000),
         name="passed_grads",
-    )(raw, raw, raw, raw_decay, raw_adjoint)
+    )(raw, raw, raw, raw, raw_adjoint)
     for group in range(RAW, G):
         grad_x = pl.pallas_call(
             place_kernel,
@@ -521,7 +527,7 @@
             out_specs=pl.BlockSpec((length, W), lambda i, group=group: (0, group)),
             out_shape=jax.ShapeDtypeStruct((length, G * W), BF16),
             input_output_aliases={1: 0},
-            compiler_params=pltpu.CompilerParams(vmem_limit_bytes=60 << 20),
+            compiler_params=pltpu.CompilerParams(vmem_limit_bytes=8 << 20),
             name="place_grads",
         )(sent[group], grad_x)
     return grad_x[None], grad_b[None], grad_c[None], grad_decay[None]

time: 117 us -> 99.8 us (0.85)
  waiting for transfers between devices: 22.1 us -> 13.6 us
  local copies, waits for them, and re-layouts: 3.94 us -> 0 us
  Pallas kernels: 81.4 us -> 78.9 us
  starting transfers between devices: 8.9 us -> 6.46 us
    ppermute x5 -> x4, waiting for transfers between devices: 22.1 us -> 13.6 us  [send(): return lax.ppermute(value, 'pipe', route)]
    unnamed x10 -> x0, local copies, waits for them, and re-layouts: 3.94 us -> none
    ppermute x5 -> x4, starting transfers between devices: 8.9 us -> 6.46 us  [send(): return lax.ppermute(value, 'pipe', route)]
    pallas_call x2, Pallas kernels: 4.12 us -> 1.86 us  [local(): pl.pallas_call(place_kernel, grid=(1,), in_specs=[pl.BlockSpec((length, W...]
  transfers between devices with their start and end apart: 5 -> 4, of which waited for: 1 -> 1; matrix products, arithmetic and copies ran while one was open for 0% -> 0% of each run, Pallas kernels for 65% -> 75%
where the time goes in v4:
time: 99.8 us; the launch traced here: 99.6 us
  Pallas kernels  78.9 us (79%)
  waiting for transfers between devices  13.6 us (14%)
  starting transfers between devices  6.46 us (6%)
    pallas_call x1, Pallas kernels, local(): pl.pallas_call(functools.partial(relay_kernel, n, halves, half), in_specs...  42.6 us
    pallas_call x3, Pallas kernels, own_groups(): pl.pallas_call(functools.partial(group_kernel, first, with_x, carried), g...  23 us
    ppermute x4, waiting for transfers between devices, send(): return lax.ppermute(value, 'pipe', route)  13.6 us
    pallas_call x1, Pallas kernels, local(): pl.pallas_call(functools.partial(passed_kernel, heads), grid=(RAW,), in_s...  8.48 us
    ppermute x4, starting transfers between devices, send(): return lax.ppermute(value, 'pipe', route)  6.46 us
    pallas_call x1, Pallas kernels, local(): pl.pallas_call(functools.partial(pack_kernel, heads), grid=(1,), in_specs...  3.01 us
  transfers between devices with their start and end apart: 4, of which 1 were waited for; matrix products, arithmetic and copies ran while one was open for 0% of the time, Pallas kernels for 75%

profile of v4, /device:TPU:0, one launch (start us, length us, event | category | flops | bytes accessed | tf_op | source)
XLA Modules:
  0.0 99.6 jit_solution(13189375551258047333)
XLA Ops:
  0.6 3.0 %pack_raw.1 = bf16[384,2688]{1,0:T(8,128)(2,1)} custom-call(bf16[384,4096]{1,0:T(8,128)(2,1)} %bitcast.9, bf16[384,512]{1,0:T(8,128)(2,1)} %bitcast.19, bf16[384,512]{1,0:T(8,128)(2,1)} %bitcast.24, f32[64,384]{1,0:T(8,128)} %bitcast.29, f32[1,64]{1,0:T(1,128)} %skip_ref.7), custom_call_target="tpu_custom_call" | custom-call | tf_op jit(solution)/shard_map/pack_raw/pallas_call | solution.py:393
  3.6 3.9 %collective-permute-start.2 = (bf16[384,2688]{1,0:T(8,128)(2,1)}, bf16[384,2688]{1,0:T(8,128)(2,1)S(1)}, u32[]{:S(2)}, u32[]{:S(2)}) collective-permute-start(bf16[384,2688]{1,0:T(8,128)(2,1)} %pack_raw.1), channel_id=1, source_target_pairs={{0,24},{8,0},{16,8},{24,16},{1,25},{9,1},{17,9},{25,17},{2,26},{10... | collective-permute-start | bytes 6193160 | tf_op jit(solution)/shard_map/ppermute | solution.py:387
  7.5 42.6 %relay.1 = (bf16[8,128,512]{2,1,0:T(8,128)(2,1)}, bf16[8,128,512]{2,1,0:T(8,128)(2,1)}, bf16[4,384,1024]{2,1,0:T(8,128)(2,1)}, f32[384,512]{1,0:T(8,128)}, f32[3...) custom-call(bf16[384,4096]{1,0:T(8,128)(2,1)} %bitcast.14, bf16[384,512]{1,0:T(8,128)(2,1)} %bitcast.20, ...), custom_call_target="tpu_custom_call" | custom-call | flops 30000001024 | bytes 8000000 | tf_op jit(solution)/shard_map/relay/pallas_call | solution.py:411
  50.1 0.6 collective-permute-start.3
  50.7 6.7 %group_grads.3 = (bf16[384,1024]{1,0:T(8,128)(2,1)}, bf16[384,512]{1,0:T(8,128)(2,1)}, bf16[384,512]{1,0:T(8,128)(2,1)}, f32[64,384]{1,0:T(8,128)}) custom-call(bf16[384,4096]{1,0:T(8,128)(2,1)} %bitcast.15, bf16[384,512]{1,0:T(8,128)(2,1)} %bitcast.21, bf16[384,512]{1,0:T(8,128)(2,1)} %bitcast.26, f32[64,384]{1,0:T(8,128)} %bitcast.31, ...), custom_call_target="tpu_custom_call" | custom-call | flops 300000000 | bytes 400000 | tf_op jit(solution)/shard_map/group_grads/pallas_call | solution.py:467
  57.4 1.4 %collective-permute-start.1 = (bf16[384,1024]{1,0:T(8,128)(2,1)}, bf16[384,1024]{1,0:T(8,128)(2,1)S(1)}, u32[]{:S(2)}, u32[]{:S(2)}) collective-permute-start(bf16[384,1024]{1,0:T(8,128)(2,1)} %get-tuple-element.32), channel_id=1, source_target_pairs={{0,24},{8,0},{16,8},{24,16},{1,25},{9,1},{17,9},{25,17},{2,26},{10... | collective-permute-start | bytes 2359304 | tf_op jit(solution)/shard_map/ppermute | solution.py:387
  58.8 6.7 %group_grads.4 = (bf16[384,1024]{1,0:T(8,128)(2,1)}, bf16[384,512]{1,0:T(8,128)(2,1)}, bf16[384,512]{1,0:T(8,128)(2,1)}, f32[64,384]{1,0:T(8,128)}) custom-call(bf16[384,4096]{1,0:T(8,128)(2,1)} %bitcast.16, bf16[384,512]{1,0:T(8,128)(2,1)} %bitcast.22, bf16[384,512]{1,0:T(8,128)(2,1)} %bitcast.27, ...), custom_call_target="tpu_custom_call", output_to_operand_aliasing={{1}: (11, {}), {2}: (12, {}), {3}: (13, {})} | custom-call | flops 300000000 | bytes 400000 | tf_op jit(solution)/shard_map/group_grads/pallas_call | solution.py:467
  65.5 0.5 collective-permute-start
  66.0 9.7 %group_grads.5 = (bf16[384,512]{1,0:T(8,128)(2,1)}, bf16[384,512]{1,0:T(8,128)(2,1)}, f32[64,384]{1,0:T(8,128)}) custom-call(bf16[384,4096]{1,0:T(8,128)(2,1)} %bitcast.17, bf16[384,512]{1,0:T(8,128)(2,1)} %bitcast.23, bf16[384,512]{1,0:T(8,128)(2,1)} %bitcast.28, f32[64,384]{1,0:T(8,128)} %bitcast.33, ...), custom_call_target="tpu_custom_call", output_to_operand_aliasing={{0}: (11, {}), {1}: (12, {}), {2}: (13, {})} | custom-call | flops 300000000 | bytes 400000 | tf_op jit(solution)/shard_map/group_grads/pallas_call | solution.py:467
  75.7 0.0 collective-permute-done.3.adj_ref
  75.7 0.0 collective-permute-done.2.g_ref.b_ref.c_ref.scalars_ref
  75.7 8.5 %passed_grads.1.whole_ref = bf16[384,4096]{1,0:T(8,128)(2,1)} custom-call(bf16[384,2688]{1,0:T(8,128)(2,1)S(1)} %collective-permute-done.2.g_ref.b_ref.c_ref.scalars_ref, bf16[384,2688]{1,0:T(8,128)(2,1)S(1)} %collective-permute-done.2.g_ref.b_ref.c_ref.scalars_ref, bf16[384,2688]{1,0:T(8,128)(2,1)S(1)} %collective-permute-done.2.g_ref.b_ref.c_ref.scalars_ref, ...), custom_call_target="tpu_custom_call" | custom-call | flops 4000000000 | bytes 400000 | tf_op jit(solution)/shard_map/passed_grads/pallas_call | solution.py:498
  84.2 0.0 collective-permute-done.1.piece_ref
  84.2 0.9 place_grads.2.whole_ref
  85.1 13.6 %collective-permute-done.piece_ref = bf16[384,1024]{1,0:T(8,128)(2,1)S(1)} collective-permute-done((bf16[384,1024]{1,0:T(8,128)(2,1)}, bf16[384,1024]{1,0:T(8,128)(2,1)S(1)}, u32[]{:S(2)}, u32[]{:S(2)}) %collective-permute-start) | collective-permute-done | bytes 786464 | tf_op jit(solution)/shard_map/ppermute | solution.py:387
  98.7 0.9 place_grads.3
Async XLA Ops:
  3.6 72.0 %collective-permute-start.2 = (bf16[384,2688]{1,0:T(8,128)(2,1)}, bf16[384,2688]{1,0:T(8,128)(2,1)S(1)}, u32[]{:S(2)}, u32[]{:S(2)}) collective-permute-start(bf16[384,2688]{1,0:T(8,128)(2,1)} %pack_raw.1), channel_id=1, source_target_pairs={{0,24},{8,0},{16,8},{24,16},{1,25},{9,1},{17,9},{25,17},{2,26},{10... | collective-permute-start | bytes 6193160 | tf_op jit(solution)/shard_map/ppermute | solution.py:387
  50.1 25.6 %collective-permute-start.3 = (bf16[4,128,512]{2,1,0:T(8,128)(2,1)}, bf16[4,128,512]{2,1,0:T(8,128)(2,1)}, u32[]{:S(2)}, u32[]{:S(2)}) collective-permute-start(bf16[4,128,512]{2,1,0:T(8,128)(2,1)} %get-tuple-element.33), channel_id=1, source_target_pairs={{0,24},{8,0},{16,8},{24,16},{1,25},{9,1},{17,9},{25,17},{2,26},{10... | collective-permute-start | bytes 1572872 | tf_op jit(solution)/shard_map/ppermute | solution.py:387
  57.4 26.8 %collective-permute-start.1 = (bf16[384,1024]{1,0:T(8,128)(2,1)}, bf16[384,1024]{1,0:T(8,128)(2,1)S(1)}, u32[]{:S(2)}, u32[]{:S(2)}) collective-permute-start(bf16[384,1024]{1,0:T(8,128)(2,1)} %get-tuple-element.32), channel_id=1, source_target_pairs={{0,24},{8,0},{16,8},{24,16},{1,25},{9,1},{17,9},{25,17},{2,26},{10... | collective-permute-start | bytes 2359304 | tf_op jit(solution)/shard_map/ppermute | solution.py:387
  65.5 33.2 %collective-permute-start = (bf16[384,1024]{1,0:T(8,128)(2,1)}, bf16[384,1024]{1,0:T(8,128)(2,1)S(1)}, u32[]{:S(2)}, u32[]{:S(2)}) collective-permute-start(bf16[384,1024]{1,0:T(8,128)(2,1)} %get-tuple-element.31), channel_id=1, source_target_pairs={{0,24},{8,0},{16,8},{24,16},{1,25},{9,1},{17,9},{25,17},{2,26},{10... | collective-permute-start | bytes 2359304 | tf_op jit(solution)/shard_map/ppermute | solution.py:387
